TPU v7x, 128 devices: a whole 4x4x4 slice. The times are simulated.
128 devices in a mesh: node: 4 (over x), dev: 32 (over y, z, core).
Axes of the slice: x: 4, y: 4, z: 4, core: 2. Of those that a mesh axis runs over, the one named last changes fastest.
Arguments:
- state: float32 [72, 8, 32768], P(None, None, ('node', 'dev')), may hold values from -6 to 6
- span_owner: int32 [32768, 1], P(('node', 'dev')), may hold values from 0 to 127; in each aligned block of 256 rows (0 to 255, 256 to 511, ...) at most 4 rows name the same one
- regime: int32 [32768], P(('node', 'dev')), may hold values from 0 to 2
- moments: float32 [72, 8, 65536], P(None, None, ('node', 'dev')), may hold values from -6 to 6
- remap_weights: float32 [512, 128, 128], P(('node', 'dev')), may hold values from -0.5 to 0.5
- remap_rows: int32 [512], P(('node', 'dev')), may hold values from 0 to 511
- remap_cols: int32 [512], P(('node', 'dev')), may hold values from 0 to 1
Outputs:
- tendencies: float32 [72, 8, 32768], P(None, None, ('node', 'dev'))
- moments_out: float32 [72, 8, 65536], P(None, None, ('node', 'dev'))
- ocean_flux: float32 [512, 4, 128], P(('node', 'dev'))
Inputs may be any that keep to these rules, and one draw needn't show every extreme that they name: `span_owner`: among the 256 columns of one device no owner is named more than 4 times; some device names some owner exactly 4 times.
All inputs are finite; a program needn't handle non-finite values.
Results may differ from a plain program's by a relative error of at most 0.00014.
Values sent between devices are 32-bit elements; how exact they have to be, the bound alone decides.
No kernel may reach another device: no remote copies, remote signals or barrier semaphores. Data moves between devices by JAX's collectives and lax.ppermute only.
A program may use at most 64 MiB of HBM per device.

v0:
```python
import jax
import jax.numpy as jnp
from jax import lax
from jax.experimental import pallas as pl
from jax.experimental.pallas import tpu as pltpu
from jax.sharding import PartitionSpec as P

LEV = 72
FLD = 8
PEERS = 128
LANES = 128
CAP = 4
COL = 256
SLOTS = CAP * PEERS
DOWN = 2
UP = 4
ROWS1 = 5
META = CAP * DOWN * LEV
ROWS_UP = CAP * UP * LEV // LANES
OCN_ROWS = 8
ROWS2 = ROWS_UP + OCN_ROWS
HALF = LEV // 2
PAD_ROWS = LEV * FLD + FLD
f32 = jnp.float32
bf16 = jnp.bfloat16


def iota(shape, axis):
    return lax.broadcasted_iota(jnp.int32, shape, axis)


def split3(x):
    hi = x.astype(bf16)
    rest = x - hi.astype(f32)
    mid = rest.astype(bf16)
    low = (rest - mid.astype(f32)).astype(bf16)
    return hi, mid, low


def columns_down(owner_row):
    real = owner_row.astype(f32)
    parts = [
        jnp.broadcast_to(real[:, h * LANES : (h + 1) * LANES], (LANES, LANES)).T
        for h in range(COL // LANES)
    ]
    return jnp.concatenate(parts, axis=0)


def pack_kernel(rows_ref, owner_ref, *refs):
    mom_refs, out_ref, block_ref = refs[:CAP], refs[CAP], refs[CAP + 1]
    owner_down = columns_down(owner_ref[...])
    peer = iota((COL, LANES), 1).astype(f32)
    count = jnp.sum((owner_down == peer).astype(f32), axis=0, keepdims=True)
    for slot in range(CAP):
        for at, moment in enumerate((0, 2)):
            first = (slot * DOWN + at) * LEV
            block_ref[first : first + LEV, :] = mom_refs[slot][pl.ds(moment, LEV, stride=FLD), :]
    tail = ROWS1 * LANES - META
    which = iota((tail, LANES), 0)
    meta = jnp.where(which == 4, jnp.broadcast_to(count, (tail, LANES)), 0.0)
    for n in range(4):
        meta = jnp.where(which == n, rows_ref[n].astype(f32), meta)
    block_ref[META:, :] = meta
    for t in range(ROWS1):
        out_ref[pl.ds(t, PEERS, stride=ROWS1), :] = block_ref[t * LANES : (t + 1) * LANES, :].T


def softplus(x):
    return jnp.maximum(x, 0.0) + jnp.log(1.0 + jnp.exp(-jnp.abs(x)))


def micro_step(x, m2, warm, mixed, above, top):
    temper, vap, liq, rain, ice = x
    vapour = softplus(vap)
    liquid = softplus(liq)
    rain_q = softplus(rain)
    ice_q = softplus(ice)
    half_t = jnp.tanh(0.5 * temper)
    satur = 0.6 * jnp.exp(0.5 * half_t)
    excess = vapour - satur
    cloudy = 1.0 + 0.5 * jnp.tanh(0.5 * (m2 + excess))
    conden = 0.4 * jnp.tanh(excess) * cloudy
    autoconv = 0.3 * liquid * liquid / (1.0 + liquid)
    evapor = 0.1 * rain_q * (0.5 - 0.5 * jnp.tanh(0.5 * excess))
    freeze = 0.3 * liquid * (0.5 - 0.5 * half_t)
    melting = 0.2 * ice_q * (0.5 + 0.5 * half_t)
    deposit = 0.35 * jnp.tanh(vapour - 0.8 * satur) * cloudy
    aggreg = 0.25 * ice_q * ice_q / (1.0 + ice_q)
    falling = 0.5 * rain_q
    rolled = pltpu.roll(falling, 1, 0)
    from_above = jnp.where(top, above, rolled)

    def pick(a, b, c):
        return jnp.where(warm, a, jnp.where(mixed, b, c))

    swap = freeze - melting
    d_temp = pick(0.8 * (conden - evapor), 0.8 * conden + 0.5 * swap, deposit + 0.5 * freeze)
    d_vap = pick(evapor - conden, -conden, -deposit)
    d_liq = pick(conden - autoconv, conden - freeze - autoconv, -freeze)
    d_rain = pick(autoconv - evapor, autoconv + melting, aggreg) + from_above - falling
    d_ice = pick(jnp.zeros_like(swap), swap, deposit + freeze - aggreg)
    new = (
        temper + 0.5 * d_temp,
        vap + 0.5 * d_vap,
        liq + 0.5 * d_liq,
        rain + 0.5 * d_rain,
        ice + 0.5 * d_ice,
    )
    return new, rolled


def solve(a_ref, k_ref, y_ref, g_ref):
    halves = range(COL // LANES)

    def kap(h, level):
        row = k_ref[level : level + 1, h * LANES : (h + 1) * LANES]
        return jnp.broadcast_to(row, (FLD, LANES))

    def rows(h, level):
        first = h * PAD_ROWS + level * FLD
        return slice(first, first + FLD)

    state = {}
    for step in range(HALF):
        for h in halves:
            for chain in range(2):
                k = LEV - 1 - step if chain else step
                k_new = kap(h, k - 1 if chain else k)
                a = a_ref[rows(h, k), :]
                if step == 0:
                    r = 1.0 / (1.0 + k_new)
                    d = a * r
                else:
                    k_old, g, d = state[h, chain]
                    r = 1.0 / (1.0 + k_new + k_old * (1.0 - g))
                    d = (a + k_old * d) * r
                g = k_new * r
                g_ref[rows(h, k), :] = g
                y_ref[rows(h, k), :] = d
                state[h, chain] = (k_new, g, d)
    z = {}
    for h in halves:
        (_, g_up, d_up), (_, g_dn, d_dn) = state[h, 0], state[h, 1]
        z[h, 0] = (d_up + g_up * d_dn) / (1.0 - g_up * g_dn)
        z[h, 1] = d_dn + g_dn * z[h, 0]
        y_ref[rows(h, HALF - 1), :] = z[h, 0]
        y_ref[rows(h, HALF), :] = z[h, 1]
    for step in range(1, HALF):
        for h in halves:
            for chain in range(2):
                k = HALF + step if chain else HALF - 1 - step
                z[h, chain] = y_ref[rows(h, k), :] + g_ref[rows(h, k), :] * z[h, chain]
                y_ref[rows(h, k), :] = z[h, chain]


def physics_kernel(
    cols_ref,
    owner_ref,
    regime_ref,
    got_ref,
    state_0,
    state_1,
    weight_ref,
    tend_out,
    out_ref,
    meta_ref,
    block_ref,
    hot_ref,
    mom_ref,
    a_ref,
    y_ref,
    g_ref,
    k_ref,
    e_ref,
    tend_ref,
    tend_sem,
):
    states = (state_0, state_1)
    owner_row = owner_ref[...]
    owner_down = columns_down(owner_row)
    owner_real = owner_row.astype(f32)
    before = jnp.zeros((1, COL), f32)
    for h in range(COL // LANES):
        same = (
            jnp.concatenate([owner_down[h * LANES : (h + 1) * LANES, :]] * 2, axis=1) == owner_real
        )
        earlier = iota((LANES, COL), 0) + h * LANES < iota((LANES, COL), 1)
        before = before + jnp.sum((same & earlier).astype(f32), axis=0, keepdims=True)
    slot = owner_row + PEERS * before.astype(jnp.int32)
    for p in range(CAP):
        hot_ref[p * PEERS : (p + 1) * PEERS, :] = (
            iota((PEERS, COL), 0) + p * PEERS == slot
        ).astype(bf16)

    for t in range(ROWS1):
        block_ref[t * LANES : (t + 1) * LANES, :] = got_ref[pl.ds(t, PEERS, stride=ROWS1), :].T
    meta_ref[...] = block_ref[META : META + 8, :]
    slotted = jnp.concatenate(
        [block_ref[p * DOWN * LEV : (p + 1) * DOWN * LEV, :] for p in range(CAP)], axis=1
    )
    total = None
    for part in split3(slotted):
        got = jnp.dot(part, hot_ref[...], preferred_element_type=f32)
        total = got if total is None else total + got
    mom_ref[0 : DOWN * LEV, :] = total

    top = iota((8, LANES), 0) == 0
    for h in range(COL // LANES):
        lanes = slice(h * LANES, (h + 1) * LANES)
        kind = regime_ref[:, lanes]
        warm = jnp.broadcast_to(kind, (8, LANES)) == 0
        mixed = jnp.broadcast_to(kind, (8, LANES)) == 1
        above = [jnp.zeros((8, LANES), f32)] * 2
        base = h * PAD_ROWS
        for i in range(LEV // 8):
            x = tuple(states[h][pl.ds(i * 64 + f, 8, stride=FLD), :] for f in range(FLD))
            x, rest = x[:5], x[5:]
            m2 = mom_ref[LEV + i * 8 : LEV + i * 8 + 8, lanes]
            for sub in range(2):
                x, above[sub] = micro_step(x, m2, warm, mixed, above[sub], top)
            for f, value in enumerate(x + rest):
                a_ref[pl.ds(base + i * 64 + f, 8, stride=FLD), :] = value
        for ref in (a_ref, y_ref):
            ref[base + LEV * FLD : base + PAD_ROWS, :] = jnp.zeros((FLD, LANES), f32)
    last = iota((8, COL), 0) == 7
    for i in range(LEV // 8):
        m0 = mom_ref[i * 8 : i * 8 + 8, :]
        m0_next = mom_ref[i * 8 + 1 : i * 8 + 9, :]
        energy = 30.5 + 30.0 * jnp.tanh(m0 + m0_next)
        if i == LEV // 8 - 1:
            energy = jnp.where(last, 0.0, energy)
        e_ref[i * 8 : i * 8 + 8, :] = energy
    for turn in range(3):
        src = a_ref if turn == 0 else y_ref
        for h in range(COL // LANES):
            lanes = slice(h * LANES, (h + 1) * LANES)
            for i in range(LEV // 8):

                def drop(f):
                    first = h * PAD_ROWS + i * 64 + f
                    return (
                        src[pl.ds(first, 8, stride=FLD), :]
                        - src[pl.ds(first + FLD, 8, stride=FLD), :]
                    )

                du, dv, dt = drop(5), drop(6), drop(0)
                shear = du * du + dv * dv
                mixing = 0.3 + 1.5 * shear / (1.0 + shear) * (0.5 - 0.5 * jnp.tanh(dt))
                k_ref[i * 8 : i * 8 + 8, lanes] = mixing * e_ref[i * 8 : i * 8 + 8, lanes]
        solve(a_ref, k_ref, y_ref, g_ref)

    field = iota((FLD, LANES), 0)
    kept = (field >= 2) & (field <= 4)
    copies = []
    for h in range(COL // LANES):
        for k in range(LEV):
            rows = slice(k * FLD, (k + 1) * FLD)
            at = slice(h * PAD_ROWS + k * FLD, h * PAD_ROWS + (k + 1) * FLD)
            mixed_state = jnp.where(kept, a_ref[at, :], y_ref[at, :])
            tend_ref[h, rows, :] = mixed_state - states[h][rows, :]
        copies.append(
            pltpu.make_async_copy(
                tend_ref.at[h], tend_out.at[:, pl.ds(h * LANES, LANES)], tend_sem.at[h]
            )
        )
        copies[-1].start()

    fields = jnp.concatenate(
        [
            jnp.concatenate(
                [y_ref[pl.ds(h * PAD_ROWS + f, LEV, stride=FLD), :] for f in (0, 1, 5, 6)], axis=0
            )
            for h in range(COL // LANES)
        ],
        axis=1,
    )
    total = None
    for part in split3(fields):
        got = lax.dot_general(
            part, hot_ref[...], (((1,), (1,)), ((), ())), preferred_element_type=f32
        )
        total = got if total is None else total + got
    for p in range(CAP):
        block_ref[p * UP * LEV : (p + 1) * UP * LEV, :] = total[:, p * PEERS : (p + 1) * PEERS]
    for t in range(ROWS_UP):
        out_ref[pl.ds(t, PEERS, stride=ROWS2), :] = block_ref[t * LANES : (t + 1) * LANES, :].T

    bottom = slice((LEV - 1) * FLD, LEV * FLD)
    b = jnp.concatenate(
        [states[h][bottom, :] + tend_ref[h, bottom, :] for h in range(COL // LANES)], axis=1
    )
    b0, b3, b5, b6 = (b[f : f + 1, :] for f in (0, 3, 5, 6))
    wind = jnp.sqrt(1.0 + b5 * b5 + b6 * b6)
    flux = jnp.concatenate(
        [
            -0.5 * wind * b5,
            -0.5 * wind * b6,
            0.5 * softplus(b3),
            -0.3 * wind * b0,
            jnp.zeros((4, COL), f32),
        ],
        axis=0,
    )
    odd = iota((PEERS, LANES), 0) % 2 == 1
    for n in range(4):
        used = jnp.where(cols_ref[n] == 0, flux[:, :LANES], flux[:, LANES:])
        product = jnp.dot(
            used, weight_ref[n], precision=lax.Precision.HIGHEST, preferred_element_type=f32
        )
        for e in range(2):
            out_ref[pl.ds(ROWS_UP + 2 * n + e, PEERS, stride=ROWS2), :] = jnp.where(
                odd, product[2 + e : 3 + e, :], product[e : e + 1, :]
            )
    for copy in copies:
        copy.wait()


def ocean_kernel(base_ref, meta_ref, got_ref, keep_ref, send_ref):
    row = iota((8, PEERS), 0)
    wanted = jnp.where(row < 4, base_ref[0] + row, base_ref[1] + row - 4).astype(f32)
    chosen = jnp.concatenate(
        [(meta_ref[n : n + 1, :] == wanted).astype(bf16) for n in range(4)], axis=1
    )
    values = jnp.concatenate(
        [
            jnp.concatenate(
                [
                    got_ref[pl.ds(ROWS_UP + 2 * n + e, PEERS, stride=ROWS2), :]
                    for e in range(2)
                ],
                axis=1,
            )
            for n in range(4)
        ],
        axis=0,
    )
    total = None
    for part in split3(values):
        got = jnp.dot(chosen, part, preferred_element_type=f32)
        total = got if total is None else total + got
    keep_ref[...] = total[0:4, :]
    send_ref[...] = total[4:8, :]


def update_kernel(meta_ref, got_ref, mom_ref, out_ref, block_ref):
    p = pl.program_id(0)

    @pl.when(p == 0)
    def unpack():
        for t in range(ROWS_UP):
            block_ref[8 + t * LANES : 8 + (t + 1) * LANES, :] = got_ref[
                pl.ds(t, PEERS, stride=ROWS2), :
            ].T

    count = meta_ref[4:5, :]
    top = iota((8, LANES), 0) == 0
    last = iota((8, LANES), 0) == 7
    live = jnp.broadcast_to(count, (8, LANES)) > p.astype(f32) + 0.5
    for i in range(LEV // 8):

        def grad(which):
            first = pl.multiple_of(8 + (p * UP + which) * LEV + i * 8, 8)
            prev = block_ref[pl.ds(first - 1, 8), :]
            after = block_ref[pl.ds(first + 1, 8), :]
            if i == 0:
                prev = jnp.where(top, block_ref[pl.ds(first, 8), :], prev)
            if i == LEV // 8 - 1:
                after = jnp.where(last, block_ref[pl.ds(first, 8), :], after)
            return prev - after

        gt, gq, gu, gv = (grad(which) for which in range(UP))
        production = (
            gu * gu + gv * gv, gt * gt, gq * gq, gt * gq, gu * gt, gv * gt, gu * gq, gu * gv,
        )
        for j in range(FLD):
            at = pl.ds(i * 64 + j, 8, stride=FLD)
            m = mom_ref[at, :]
            new = m + 0.5 * (jnp.tanh(production[j]) - (0.3 + 0.1 * j) * m)
            out_ref[at, :] = jnp.where(live, new, m)


SMEM = pl.BlockSpec(memory_space=pltpu.SMEM)
VMEM = pl.BlockSpec(memory_space=pltpu.VMEM)


def lane_tile(rows, tile):
    return pl.BlockSpec((rows, LANES), lambda *_: (0, tile))


def call(kernel, grid, ins, outs, out_specs, scratch, name):
    return pl.pallas_call(
        kernel,
        grid=grid,
        in_specs=ins,
        out_specs=out_specs,
        out_shape=[jax.ShapeDtypeStruct(shape, f32) for shape in outs],
        scratch_shapes=scratch,
        name=name,
    )


def pack(rows, owner_row, mom):
    return call(
        pack_kernel,
        (1,),
        [SMEM, VMEM] + [lane_tile(LEV * FLD, p) for p in range(CAP)],
        [(ROWS1 * PEERS, LANES)],
        [VMEM],
        [pltpu.VMEM((ROWS1 * LANES, LANES), f32)],
        "pack",
    )(rows, owner_row, *[mom] * CAP)[0]


def physics(cols, owner_row, regime_row, got, state, weights):
    rows = LEV * FLD
    return call(
        physics_kernel,
        (1,),
        [SMEM] + [VMEM] * 3 + [lane_tile(rows, h) for h in range(COL // LANES)] + [VMEM],
        [(rows, COL), (ROWS2 * PEERS, LANES), (8, PEERS)],
        [pl.BlockSpec(memory_space=pl.ANY), VMEM, VMEM],
        [
            pltpu.VMEM((ROWS_UP * LANES, LANES), f32),
            pltpu.VMEM((SLOTS, COL), bf16),
            pltpu.VMEM((DOWN * LEV + 8, COL), f32),
            pltpu.VMEM((2 * PAD_ROWS, LANES), f32),
            pltpu.VMEM((2 * PAD_ROWS, LANES), f32),
            pltpu.VMEM((2 * PAD_ROWS, LANES), f32),
            pltpu.VMEM((LEV, COL), f32),
            pltpu.VMEM((LEV, COL), f32),
            pltpu.VMEM((2, rows, LANES), f32),
            pltpu.SemaphoreType.DMA((2,)),
        ],
        "physics",
    )(cols, owner_row, regime_row, got, state, state, weights)


def ocean(*args):
    return call(
        ocean_kernel, (1,), [SMEM, VMEM, VMEM], [(4, 2 * LANES)] * 2, [VMEM] * 2, [], "ocean"
    )(*args)


def update(meta, back, mom):
    block = pl.BlockSpec((LEV * FLD, LANES), lambda p: (0, p))
    return call(
        update_kernel,
        (CAP,),
        [VMEM, VMEM, block],
        [(LEV * FLD, SLOTS)],
        [block],
        [pltpu.VMEM((ROWS_UP * LANES + 16, LANES), f32)],
        "update",
    )(meta, back, mom)[0]


def exchange(sent, rows):
    got = lax.all_to_all(
        sent.reshape(PEERS, 1, rows * LANES), ("node", "dev"), 0, 0, tiled=True
    )
    return got.reshape(PEERS * rows, LANES)


def local(state, span_owner, regime, moments, remap_weights, remap_rows, remap_cols):
    dev_count = lax.axis_size("dev")
    core = lax.axis_index("dev") % 2
    device = lax.axis_index(("node", "dev"))
    owner_row = span_owner.reshape(1, COL)
    mom = moments.reshape(LEV * FLD, SLOTS)
    got = exchange(pack(remap_rows, owner_row, mom), ROWS1)
    tend, sent, meta = physics(
        remap_cols, owner_row, regime.reshape(1, COL), got, state.reshape(LEV * FLD, COL), remap_weights
    )
    back = exchange(sent, ROWS2)
    base = jnp.stack([device * 4, (device + 1 - 2 * core) * 4]).astype(jnp.int32)
    keep, send = ocean(base, meta, back)
    other = lax.ppermute(send, "dev", [(i, i ^ 1) for i in range(dev_count)])
    new_mom = update(meta, back, mom)
    low = jnp.where(core == 0, keep, other).reshape(4, 2, LANES)
    high = jnp.where(core == 0, other, keep).reshape(4, 2, LANES)
    return (
        tend.reshape(LEV, FLD, COL),
        new_mom.reshape(LEV, FLD, SLOTS),
        jnp.concatenate([low, high], axis=1),
    )


def solution(mesh):
    return jax.shard_map(
        local,
        mesh=mesh,
        in_specs=(
            P(None, None, ("node", "dev")),
            P(("node", "dev"), None),
            P(("node", "dev")),
            P(None, None, ("node", "dev")),
            P(("node", "dev"), None, None),
            P(("node", "dev")),
            P(("node", "dev")),
        ),
        out_specs=(
            P(None, None, ("node", "dev")),
            P(None, None, ("node", "dev")),
            P(("node", "dev"), None, None),
        ),
        check_vma=False,
    )
```

profile of v0, /device:TPU:1, one launch (start us, length us, event | category | flops | bytes accessed | tf_op | source)
XLA Modules:
  0.0 65.6 jit_solution(14217533370387684119)
XLA Ops:
  0.6 2.2 %pack.1 = f32[640,128]{1,0:T(8,128)} custom-call(s32[4]{0:T(128)} %rows_ref.1, s32[1,256]{1,0:T(1,128)} %bitcast.25, f32[576,512]{1,0:T(8,128)} %bitcast.12, f32[576,512]{1,0:T(8,128)} %bitcast.13, f32[576,512]{1,0:T(8,128)} %bitcast.14, f32[576,512]{1,0:T(8,128)} %bitcast.15), custom_call_target="tpu_custom_call" | custom-call | tf_op jit(solution)/shard_map/pack/pallas_call | solution.py:403
  2.8 23.1 %all_to_all.10 = f32[128,1,640]{2,1,0:T(1,128)} all-to-all(f32[128,1,640]{2,1,0:T(1,128)} %bitcast.21), channel_id=1, replica_groups=mesh['node'=4,'dev'=32] {'node','dev'}, dimensions={0} | all-to-all | bytes 655360 | tf_op jit(solution)/shard_map/all_to_all | solution.py:458
  25.9 5.8 %physics.1 = (f32[576,256]{1,0:T(8,128)}, f32[2176,128]{1,0:T(8,128)}, f32[8,128]{1,0:T(8,128)}) custom-call(s32[4]{0:T(128)} %cols_ref.1, s32[1,256]{1,0:T(1,128)} %bitcast.26, s32[1,256]{1,0:T(1,128)} %bitcast.27, f32[640,128]{1,0:T(8,128)} %bitcast.22, f32[576,256]{1,0:T(8,128)} %bitcast.19, f32[576,256]{1,0:T(8,128)} %bitcast.20, f32[4,128,128]{2,1,0:T(8,128)} %weight_ref.1), custom_call_target="tpu_custom_call" | custom-call | tf_op jit(solution)/shard_map/physics/pallas_call | solution.py:416
  31.7 4.8 %all-to-all-start.1 = ((f32[128,1,2176]{2,1,0:T(1,128)}), f32[128,1,2176]{2,1,0:T(1,128)S(1)}, u32[]{:S(2)}, u32[]{:S(2)}) async-start(f32[128,1,2176]{2,1,0:T(1,128)} %bitcast.24), calls=%async_computation.1 | async-start | bytes 2228224 | tf_op jit(solution)/shard_map/all_to_all | solution.py:458
  36.5 0.6 pad_add_fusion.base_ref
  37.0 19.3 %all-to-all-done.1 = f32[128,1,2176]{2,1,0:T(1,128)S(1)} async-done(((f32[128,1,2176]{2,1,0:T(1,128)}), f32[128,1,2176]{2,1,0:T(1,128)S(1)}, u32[]{:S(2)}, u32[]{:S(2)}) %all-to-all-start.1) | async-done | bytes 1114144 | tf_op jit(solution)/shard_map/all_to_all | solution.py:458
  56.4 0.0 copy-start
  56.4 1.0 %copy-done = f32[128,1,2176]{2,1,0:T(1,128)} copy-done((f32[128,1,2176]{2,1,0:T(1,128)}, f32[128,1,2176]{2,1,0:T(1,128)S(1)}, u32[]{:S(2)}) %copy-start) | copy-done | bytes 1114136
  57.4 2.1 %ocean.1 = (f32[4,256]{1,0:T(4,128)}, f32[4,256]{1,0:T(4,128)}) custom-call(s32[2]{0:T(128)} %pad_add_fusion.base_ref, f32[8,128]{1,0:T(8,128)} %get-tuple-element.9.meta_ref, f32[2176,128]{1,0:T(8,128)} %bitcast.17), custom_call_target="tpu_custom_call" | custom-call | tf_op jit(solution)/shard_map/ocean/pallas_call | solution.py:439
  59.5 1.3 %collective-permute-start = (f32[4,256]{1,0:T(4,128)}, f32[4,256]{1,0:T(4,128)S(1)}, u32[]{:S(2)}, u32[]{:S(2)}) collective-permute-start(f32[4,256]{1,0:T(4,128)} %get-tuple-element.12), channel_id=1, source_target_pairs={{0,1},{1,0},{2,3},{3,2},{4,5},{5,4},{6,7},{7,6},{8,9},{9,8},{10,11... | collective-permute-start | bytes 12296 | tf_op jit(solution)/shard_map/ppermute | solution.py:477
  60.7 0.0 copy-start.1
  60.7 4.2 %update.1 = f32[576,512]{1,0:T(8,128)} custom-call(f32[8,128]{1,0:T(8,128)} %get-tuple-element.9.meta_ref, f32[2176,128]{1,0:T(8,128)} %bitcast.18, f32[576,512]{1,0:T(8,128)} %bitcast.16), custom_call_target="tpu_custom_call" | custom-call | tf_op jit(solution)/shard_map/update/pallas_call | solution.py:446
  65.0 0.0 collective-permute-done
  65.0 0.0 copy-done.1
  65.0 0.6 pad_maximum_fusion
  (3 shorter events, 0.0 us)
Async XLA Ops:
  31.7 24.7 %all-to-all-start.1 = ((f32[128,1,2176]{2,1,0:T(1,128)}), f32[128,1,2176]{2,1,0:T(1,128)S(1)}, u32[]{:S(2)}, u32[]{:S(2)}) async-start(f32[128,1,2176]{2,1,0:T(1,128)} %bitcast.24), calls=%async_computation.1 | async-start | bytes 2228224 | tf_op jit(solution)/shard_map/all_to_all | solution.py:458
  56.4 1.0 %copy-start = (f32[128,1,2176]{2,1,0:T(1,128)}, f32[128,1,2176]{2,1,0:T(1,128)S(1)}, u32[]{:S(2)}) copy-start(f32[128,1,2176]{2,1,0:T(1,128)S(1)} %all-to-all-done.1) | copy-start | bytes 3342340
  59.5 5.5 %collective-permute-start = (f32[4,256]{1,0:T(4,128)}, f32[4,256]{1,0:T(4,128)S(1)}, u32[]{:S(2)}, u32[]{:S(2)}) collective-permute-start(f32[4,256]{1,0:T(4,128)} %get-tuple-element.12), channel_id=1, source_target_pairs={{0,1},{1,0},{2,3},{3,2},{4,5},{5,4},{6,7},{7,6},{8,9},{9,8},{10,11... | collective-permute-start | bytes 12296 | tf_op jit(solution)/shard_map/ppermute | solution.py:477
  60.7 4.2 %copy-start.1 = (f32[4,256]{1,0:T(4,128)S(1)}, f32[4,256]{1,0:T(4,128)}, u32[]{:S(2)}) copy-start(f32[4,256]{1,0:T(4,128)} %get-tuple-element.11) | copy-start | bytes 12292
where the time goes:
time: 66 us; the launch traced here: 65.6 us
  blocking collectives  23.1 us (35%)
  waiting for transfers between devices  19.3 us (29%)
  Pallas kernels  14.4 us (22%)
  starting transfers between devices  6.01 us (9%)
  other arithmetic  1.19 us (2%)
  local copies, waits for them, and re-layouts  1.02 us (2%)
  between operations  0.68 us (1%)
    all_to_all x1, blocking collectives, exchange(): lax.all_to_all(sent.reshape(PEERS, 1, rows * LANES), ('node', 'dev'), 0,...  23.1 us
    all_to_all x1, waiting for transfers between devices, exchange(): lax.all_to_all(sent.reshape(PEERS, 1, rows * LANES), ('node', 'dev'), 0,...  19.3 us
    pallas_call x1, Pallas kernels, physics(): call(physics_kernel, (1,), [SMEM] + [VMEM] * 3 + [lane_tile(rows, h) for...  5.79 us
    all_to_all x1, starting transfers between devices, exchange(): lax.all_to_all(sent.reshape(PEERS, 1, rows * LANES), ('node', 'dev'), 0,...  4.75 us
    pallas_call x1, Pallas kernels, update(): call(update_kernel, (CAP,), [VMEM, VMEM, block], [(LEV * FLD, SLOTS)], [b...  4.24 us
    pallas_call x1, Pallas kernels, pack(): call(pack_kernel, (1,), [SMEM, VMEM] + [lane_tile(LEV * FLD, p) for p in...  2.21 us
    pallas_call x1, Pallas kernels, ocean(): call(ocean_kernel, (1,), [SMEM, VMEM, VMEM], [(4, 2 * LANES)] * 2, [VMEM]...  2.11 us
  transfers between devices with their start and end apart: 2, of which 1 were waited for; matrix products, arithmetic and copies ran while one was open for 1% of the time, Pallas kernels for 6%

commit v1 on v0

--- a/solution.py
+++ b/solution.py
@@ -46,21 +46,39 @@
     return jnp.concatenate(parts, axis=0)
 
 
-def pack_kernel(rows_ref, owner_ref, *refs):
-    mom_refs, out_ref, block_ref = refs[:CAP], refs[CAP], refs[CAP + 1]
+def pack_kernel(
+    rows_hbm, owner_hbm, mom_ref, out_ref, tile_ref, rows_ref, owner_ref, block_ref, sem, small_sem
+):
+    small = [
+        pltpu.make_async_copy(owner_hbm, owner_ref, small_sem.at[0]),
+        pltpu.make_async_copy(rows_hbm, rows_ref, small_sem.at[1]),
+    ]
+    for copy in small:
+        copy.start()
+    copies = [
+        pltpu.make_async_copy(
+            mom_ref.at[:, pl.ds(p * LANES, LANES)], tile_ref.at[p], sem.at[p]
+        )
+        for p in range(CAP)
+    ]
+    for copy in copies:
+        copy.start()
+    for copy in small:
+        copy.wait()
     owner_down = columns_down(owner_ref[...])
     peer = iota((COL, LANES), 1).astype(f32)
     count = jnp.sum((owner_down == peer).astype(f32), axis=0, keepdims=True)
-    for slot in range(CAP):
-        for at, moment in enumerate((0, 2)):
-            first = (slot * DOWN + at) * LEV
-            block_ref[first : first + LEV, :] = mom_refs[slot][pl.ds(moment, LEV, stride=FLD), :]
     tail = ROWS1 * LANES - META
     which = iota((tail, LANES), 0)
     meta = jnp.where(which == 4, jnp.broadcast_to(count, (tail, LANES)), 0.0)
     for n in range(4):
         meta = jnp.where(which == n, rows_ref[n].astype(f32), meta)
     block_ref[META:, :] = meta
+    for p in range(CAP):
+        copies[p].wait()
+        for at, moment in enumerate((0, 2)):
+            first = (p * DOWN + at) * LEV
+            block_ref[first : first + LEV, :] = tile_ref[p, pl.ds(moment, LEV, stride=FLD), :]
     for t in range(ROWS1):
         out_ref[pl.ds(t, PEERS, stride=ROWS1), :] = block_ref[t * LANES : (t + 1) * LANES, :].T
 
@@ -69,7 +87,7 @@
     return jnp.maximum(x, 0.0) + jnp.log(1.0 + jnp.exp(-jnp.abs(x)))
 
 
-def micro_step(x, m2, warm, mixed, above, top):
+def micro_free(x, warm, mixed, icy, above, top):
     temper, vap, liq, rain, ice = x
     vapour = softplus(vap)
     liquid = softplus(liq)
@@ -78,35 +96,43 @@
     half_t = jnp.tanh(0.5 * temper)
     satur = 0.6 * jnp.exp(0.5 * half_t)
     excess = vapour - satur
-    cloudy = 1.0 + 0.5 * jnp.tanh(0.5 * (m2 + excess))
-    conden = 0.4 * jnp.tanh(excess) * cloudy
     autoconv = 0.3 * liquid * liquid / (1.0 + liquid)
     evapor = 0.1 * rain_q * (0.5 - 0.5 * jnp.tanh(0.5 * excess))
     freeze = 0.3 * liquid * (0.5 - 0.5 * half_t)
     melting = 0.2 * ice_q * (0.5 + 0.5 * half_t)
-    deposit = 0.35 * jnp.tanh(vapour - 0.8 * satur) * cloudy
     aggreg = 0.25 * ice_q * ice_q / (1.0 + ice_q)
     falling = 0.5 * rain_q
     rolled = pltpu.roll(falling, 1, 0)
     from_above = jnp.where(top, above, rolled)
+    source = jnp.where(
+        icy, 0.175 * jnp.tanh(vapour - 0.8 * satur), 0.2 * jnp.tanh(excess)
+    )
 
     def pick(a, b, c):
         return jnp.where(warm, a, jnp.where(mixed, b, c))
 
     swap = freeze - melting
-    d_temp = pick(0.8 * (conden - evapor), 0.8 * conden + 0.5 * swap, deposit + 0.5 * freeze)
-    d_vap = pick(evapor - conden, -conden, -deposit)
-    d_liq = pick(conden - autoconv, conden - freeze - autoconv, -freeze)
-    d_rain = pick(autoconv - evapor, autoconv + melting, aggreg) + from_above - falling
-    d_ice = pick(jnp.zeros_like(swap), swap, deposit + freeze - aggreg)
-    new = (
-        temper + 0.5 * d_temp,
-        vap + 0.5 * d_vap,
-        liq + 0.5 * d_liq,
-        rain + 0.5 * d_rain,
-        ice + 0.5 * d_ice,
-    )
-    return new, rolled
+    kept = (
+        temper + pick(-0.4 * evapor, 0.25 * swap, 0.25 * freeze),
+        jnp.where(warm, vap + 0.5 * evapor, vap),
+        liq - 0.5 * pick(autoconv, freeze + autoconv, freeze),
+        rain
+        + 0.5 * (pick(autoconv - evapor, autoconv + melting, aggreg) + from_above - falling),
+        jnp.where(warm, ice, ice + 0.5 * jnp.where(mixed, swap, freeze - aggreg)),
+    )
+    return kept, source, excess, rolled
+
+
+def micro_bound(kept, source, excess, m2, icy):
+    temper, vap, liq, rain, ice = kept
+    gain = source * (1.0 + 0.5 * jnp.tanh(0.5 * (m2 + excess)))
+    return (
+        temper + jnp.where(icy, gain, 0.8 * gain),
+        vap - gain,
+        jnp.where(icy, liq, liq + gain),
+        rain,
+        jnp.where(icy, ice + gain, ice),
+    )
 
 
 def solve(a_ref, k_ref, y_ref, g_ref):
@@ -153,29 +179,22 @@
                 y_ref[rows(h, k), :] = z[h, chain]
 
 
-def physics_kernel(
-    cols_ref,
-    owner_ref,
-    regime_ref,
-    got_ref,
-    state_0,
-    state_1,
-    weight_ref,
-    tend_out,
-    out_ref,
-    meta_ref,
-    block_ref,
-    hot_ref,
-    mom_ref,
-    a_ref,
-    y_ref,
-    g_ref,
-    k_ref,
-    e_ref,
-    tend_ref,
-    tend_sem,
+def regimes(regime_ref, h):
+    kind = jnp.broadcast_to(regime_ref[:, h * LANES : (h + 1) * LANES], (8, LANES))
+    return kind == 0, kind == 1, kind == 2
+
+
+def prepare_kernel(
+    owner_ref, regime_ref, state_ref, tile_ref, hot_ref, part_ref, sem
 ):
-    states = (state_0, state_1)
+    copies = [
+        pltpu.make_async_copy(
+            state_ref.at[:, pl.ds(h * LANES, LANES)], tile_ref.at[h], sem.at[h]
+        )
+        for h in range(COL // LANES)
+    ]
+    for copy in copies:
+        copy.start()
     owner_row = owner_ref[...]
     owner_down = columns_down(owner_row)
     owner_real = owner_row.astype(f32)
@@ -191,7 +210,43 @@
         hot_ref[p * PEERS : (p + 1) * PEERS, :] = (
             iota((PEERS, COL), 0) + p * PEERS == slot
         ).astype(bf16)
-
+    top = iota((8, LANES), 0) == 0
+    for h in range(COL // LANES):
+        copies[h].wait()
+        warm, mixed, icy = regimes(regime_ref, h)
+        above = jnp.zeros((8, LANES), f32)
+        for i in range(LEV // 8):
+            x = tuple(tile_ref[h, pl.ds(i * 64 + f, 8, stride=FLD), :] for f in range(5))
+            kept, source, excess, above = micro_free(x, warm, mixed, icy, above, top)
+            for f, value in enumerate(kept + (source, excess)):
+                part_ref[h, f, i * 8 : i * 8 + 8, :] = value
+
+
+def physics_kernel(
+    cols_ref,
+    regime_ref,
+    got_ref,
+    tile_ref,
+    hot_ref,
+    part_ref,
+    weight_hbm,
+    tend_out,
+    out_ref,
+    meta_ref,
+    weight_ref,
+    tend_ref,
+    block_ref,
+    mom_ref,
+    a_ref,
+    y_ref,
+    g_ref,
+    k_ref,
+    e_ref,
+    weight_sem,
+    tend_sem,
+):
+    weights = pltpu.make_async_copy(weight_hbm, weight_ref, weight_sem)
+    weights.start()
     for t in range(ROWS1):
         block_ref[t * LANES : (t + 1) * LANES, :] = got_ref[pl.ds(t, PEERS, stride=ROWS1), :].T
     meta_ref[...] = block_ref[META : META + 8, :]
@@ -207,19 +262,21 @@
     top = iota((8, LANES), 0) == 0
     for h in range(COL // LANES):
         lanes = slice(h * LANES, (h + 1) * LANES)
-        kind = regime_ref[:, lanes]
-        warm = jnp.broadcast_to(kind, (8, LANES)) == 0
-        mixed = jnp.broadcast_to(kind, (8, LANES)) == 1
-        above = [jnp.zeros((8, LANES), f32)] * 2
+        warm, mixed, icy = regimes(regime_ref, h)
+        above = jnp.zeros((8, LANES), f32)
         base = h * PAD_ROWS
         for i in range(LEV // 8):
-            x = tuple(states[h][pl.ds(i * 64 + f, 8, stride=FLD), :] for f in range(FLD))
-            x, rest = x[:5], x[5:]
             m2 = mom_ref[LEV + i * 8 : LEV + i * 8 + 8, lanes]
-            for sub in range(2):
-                x, above[sub] = micro_step(x, m2, warm, mixed, above[sub], top)
-            for f, value in enumerate(x + rest):
+            first = tuple(part_ref[h, f, i * 8 : i * 8 + 8, :] for f in range(7))
+            x = micro_bound(first[:5], first[5], first[6], m2, icy)
+            kept, source, excess, above = micro_free(x, warm, mixed, icy, above, top)
+            x = micro_bound(kept, source, excess, m2, icy)
+            for f, value in enumerate(x):
                 a_ref[pl.ds(base + i * 64 + f, 8, stride=FLD), :] = value
+            for f in range(5, FLD):
+                a_ref[pl.ds(base + i * 64 + f, 8, stride=FLD), :] = tile_ref[
+                    h, pl.ds(i * 64 + f, 8, stride=FLD), :
+                ]
         for ref in (a_ref, y_ref):
             ref[base + LEV * FLD : base + PAD_ROWS, :] = jnp.zeros((FLD, LANES), f32)
     last = iota((8, COL), 0) == 7
@@ -257,7 +314,7 @@
             rows = slice(k * FLD, (k + 1) * FLD)
             at = slice(h * PAD_ROWS + k * FLD, h * PAD_ROWS + (k + 1) * FLD)
             mixed_state = jnp.where(kept, a_ref[at, :], y_ref[at, :])
-            tend_ref[h, rows, :] = mixed_state - states[h][rows, :]
+            tend_ref[h, rows, :] = mixed_state - tile_ref[h, rows, :]
         copies.append(
             pltpu.make_async_copy(
                 tend_ref.at[h], tend_out.at[:, pl.ds(h * LANES, LANES)], tend_sem.at[h]
@@ -287,7 +344,7 @@
 
     bottom = slice((LEV - 1) * FLD, LEV * FLD)
     b = jnp.concatenate(
-        [states[h][bottom, :] + tend_ref[h, bottom, :] for h in range(COL // LANES)], axis=1
+        [tile_ref[h, bottom, :] + tend_ref[h, bottom, :] for h in range(COL // LANES)], axis=1
     )
     b0, b3, b5, b6 = (b[f : f + 1, :] for f in (0, 3, 5, 6))
     wind = jnp.sqrt(1.0 + b5 * b5 + b6 * b6)
@@ -302,6 +359,7 @@
         axis=0,
     )
     odd = iota((PEERS, LANES), 0) % 2 == 1
+    weights.wait()
     for n in range(4):
         used = jnp.where(cols_ref[n] == 0, flux[:, :LANES], flux[:, LANES:])
         product = jnp.dot(
@@ -342,116 +400,158 @@
     send_ref[...] = total[4:8, :]
 
 
-def update_kernel(meta_ref, got_ref, mom_ref, out_ref, block_ref):
-    p = pl.program_id(0)
-
-    @pl.when(p == 0)
-    def unpack():
-        for t in range(ROWS_UP):
-            block_ref[8 + t * LANES : 8 + (t + 1) * LANES, :] = got_ref[
-                pl.ds(t, PEERS, stride=ROWS2), :
-            ].T
-
+def update_kernel(meta_ref, got_ref, tile_ref, out_ref, block_ref, new_ref, sem):
+    for t in range(ROWS_UP):
+        block_ref[8 + t * LANES : 8 + (t + 1) * LANES, :] = got_ref[
+            pl.ds(t, PEERS, stride=ROWS2), :
+        ].T
     count = meta_ref[4:5, :]
     top = iota((8, LANES), 0) == 0
     last = iota((8, LANES), 0) == 7
-    live = jnp.broadcast_to(count, (8, LANES)) > p.astype(f32) + 0.5
-    for i in range(LEV // 8):
-
-        def grad(which):
-            first = pl.multiple_of(8 + (p * UP + which) * LEV + i * 8, 8)
-            prev = block_ref[pl.ds(first - 1, 8), :]
-            after = block_ref[pl.ds(first + 1, 8), :]
-            if i == 0:
-                prev = jnp.where(top, block_ref[pl.ds(first, 8), :], prev)
-            if i == LEV // 8 - 1:
-                after = jnp.where(last, block_ref[pl.ds(first, 8), :], after)
-            return prev - after
-
-        gt, gq, gu, gv = (grad(which) for which in range(UP))
-        production = (
-            gu * gu + gv * gv, gt * gt, gq * gq, gt * gq, gu * gt, gv * gt, gu * gq, gu * gv,
+    copies = []
+    for p in range(CAP):
+        live = jnp.broadcast_to(count, (8, LANES)) > p + 0.5
+        for i in range(LEV // 8):
+
+            def grad(which):
+                first = 8 + (p * UP + which) * LEV + i * 8
+                prev = block_ref[first - 1 : first + 7, :]
+                after = block_ref[first + 1 : first + 9, :]
+                if i == 0:
+                    prev = jnp.where(top, block_ref[first : first + 8, :], prev)
+                if i == LEV // 8 - 1:
+                    after = jnp.where(last, block_ref[first : first + 8, :], after)
+                return prev - after
+
+            gt, gq, gu, gv = (grad(which) for which in range(UP))
+            production = (
+                gu * gu + gv * gv, gt * gt, gq * gq, gt * gq, gu * gt, gv * gt, gu * gq, gu * gv,
+            )
+            for j in range(FLD):
+                at = pl.ds(i * 64 + j, 8, stride=FLD)
+                m = tile_ref[p, at, :]
+                new = m + 0.5 * (jnp.tanh(production[j]) - (0.3 + 0.1 * j) * m)
+                new_ref[p, at, :] = jnp.where(live, new, m)
+        copies.append(
+            pltpu.make_async_copy(
+                new_ref.at[p], out_ref.at[:, pl.ds(p * LANES, LANES)], sem.at[p]
+            )
         )
-        for j in range(FLD):
-            at = pl.ds(i * 64 + j, 8, stride=FLD)
-            m = mom_ref[at, :]
-            new = m + 0.5 * (jnp.tanh(production[j]) - (0.3 + 0.1 * j) * m)
-            out_ref[at, :] = jnp.where(live, new, m)
+        copies[-1].start()
+    for copy in copies:
+        copy.wait()
 
 
 SMEM = pl.BlockSpec(memory_space=pltpu.SMEM)
 VMEM = pl.BlockSpec(memory_space=pltpu.VMEM)
-
-
-def lane_tile(rows, tile):
-    return pl.BlockSpec((rows, LANES), lambda *_: (0, tile))
-
-
-def call(kernel, grid, ins, outs, out_specs, scratch, name):
+ANY = pl.BlockSpec(memory_space=pl.ANY)
+HBM = pl.BlockSpec(memory_space=pltpu.HBM)
+PLANE = LEV * FLD
+VMEM_LIMIT = 16 << 20
+
+
+def here(shape, dtype=f32):
+    return pltpu.VMEM(shape, dtype)
+
+
+def far(shape):
+    return jax.ShapeDtypeStruct(shape, f32)
+
+
+def hold(x):
+    return pltpu.with_memory_space_constraint(x, pltpu.VMEM)
+
+
+def outside(x):
+    return pltpu.with_memory_space_constraint(x, pltpu.HBM)
+
+
+def call(kernel, ins, outs, out_specs, scratch, name):
     return pl.pallas_call(
         kernel,
-        grid=grid,
         in_specs=ins,
         out_specs=out_specs,
-        out_shape=[jax.ShapeDtypeStruct(shape, f32) for shape in outs],
+        out_shape=outs,
         scratch_shapes=scratch,
         name=name,
+        compiler_params=pltpu.CompilerParams(vmem_limit_bytes=VMEM_LIMIT),
     )
 
 
 def pack(rows, owner_row, mom):
     return call(
         pack_kernel,
-        (1,),
-        [SMEM, VMEM] + [lane_tile(LEV * FLD, p) for p in range(CAP)],
-        [(ROWS1 * PEERS, LANES)],
-        [VMEM],
-        [pltpu.VMEM((ROWS1 * LANES, LANES), f32)],
+        [HBM] * 3,
+        [here((ROWS1 * PEERS, LANES)), here((CAP, PLANE, LANES))],
+        [VMEM] * 2,
+        [
+            pltpu.SMEM((4,), jnp.int32),
+            pltpu.VMEM((1, COL), jnp.int32),
+            pltpu.VMEM((ROWS1 * LANES, LANES), f32),
+            pltpu.SemaphoreType.DMA((CAP,)),
+            pltpu.SemaphoreType.DMA((2,)),
+        ],
         "pack",
-    )(rows, owner_row, *[mom] * CAP)[0]
-
-
-def physics(cols, owner_row, regime_row, got, state, weights):
-    rows = LEV * FLD
+    )(outside(rows), outside(owner_row), outside(mom))
+
+
+def prepare(owner_row, regime_row, state):
+    return call(
+        prepare_kernel,
+        [VMEM, VMEM, HBM],
+        [
+            here((2, PLANE, LANES)),
+            here((SLOTS, COL), bf16),
+            here((2, 7, LEV, LANES)),
+        ],
+        [VMEM] * 3,
+        [pltpu.SemaphoreType.DMA((2,))],
+        "prepare",
+    )(owner_row, regime_row, outside(state))
+
+
+def physics(cols, regime_row, got, tiles, hot, parts, weights):
     return call(
         physics_kernel,
-        (1,),
-        [SMEM] + [VMEM] * 3 + [lane_tile(rows, h) for h in range(COL // LANES)] + [VMEM],
-        [(rows, COL), (ROWS2 * PEERS, LANES), (8, PEERS)],
-        [pl.BlockSpec(memory_space=pl.ANY), VMEM, VMEM],
+        [SMEM] + [VMEM] * 5 + [HBM],
+        [far((PLANE, COL)), here((ROWS2 * PEERS, LANES)), here((8, PEERS))],
+        [ANY, VMEM, VMEM],
         [
+            pltpu.VMEM((4, LANES, LANES), f32),
+            pltpu.VMEM((2, PLANE, LANES), f32),
             pltpu.VMEM((ROWS_UP * LANES, LANES), f32),
-            pltpu.VMEM((SLOTS, COL), bf16),
             pltpu.VMEM((DOWN * LEV + 8, COL), f32),
             pltpu.VMEM((2 * PAD_ROWS, LANES), f32),
             pltpu.VMEM((2 * PAD_ROWS, LANES), f32),
             pltpu.VMEM((2 * PAD_ROWS, LANES), f32),
             pltpu.VMEM((LEV, COL), f32),
             pltpu.VMEM((LEV, COL), f32),
-            pltpu.VMEM((2, rows, LANES), f32),
+            pltpu.SemaphoreType.DMA,
             pltpu.SemaphoreType.DMA((2,)),
         ],
         "physics",
-    )(cols, owner_row, regime_row, got, state, state, weights)
-
-
-def ocean(*args):
+    )(cols, regime_row, *(hold(x) for x in (got, tiles, hot, parts)), outside(weights))
+
+
+def ocean(base, meta, back):
     return call(
-        ocean_kernel, (1,), [SMEM, VMEM, VMEM], [(4, 2 * LANES)] * 2, [VMEM] * 2, [], "ocean"
-    )(*args)
-
-
-def update(meta, back, mom):
-    block = pl.BlockSpec((LEV * FLD, LANES), lambda p: (0, p))
+        ocean_kernel, [SMEM, VMEM, VMEM], [here((4, 2 * LANES))] * 2, [VMEM] * 2, [], "ocean"
+    )(base, hold(meta), hold(back))
+
+
+def update(meta, back, tiles):
     return call(
         update_kernel,
-        (CAP,),
-        [VMEM, VMEM, block],
-        [(LEV * FLD, SLOTS)],
-        [block],
-        [pltpu.VMEM((ROWS_UP * LANES + 16, LANES), f32)],
+        [VMEM] * 3,
+        [far((PLANE, SLOTS))],
+        [ANY],
+        [
+            pltpu.VMEM((ROWS_UP * LANES + 16, LANES), f32),
+            pltpu.VMEM((CAP, PLANE, LANES), f32),
+            pltpu.SemaphoreType.DMA((CAP,)),
+        ],
         "update",
-    )(meta, back, mom)[0]
+    )(hold(meta), hold(back), hold(tiles))[0]
 
 
 def exchange(sent, rows):
@@ -466,16 +566,16 @@
     core = lax.axis_index("dev") % 2
     device = lax.axis_index(("node", "dev"))
     owner_row = span_owner.reshape(1, COL)
-    mom = moments.reshape(LEV * FLD, SLOTS)
-    got = exchange(pack(remap_rows, owner_row, mom), ROWS1)
-    tend, sent, meta = physics(
-        remap_cols, owner_row, regime.reshape(1, COL), got, state.reshape(LEV * FLD, COL), remap_weights
-    )
+    regime_row = regime.reshape(1, COL)
+    sent, mom_tiles = pack(remap_rows, owner_row, moments.reshape(PLANE, SLOTS))
+    tiles, hot, parts = prepare(owner_row, regime_row, state.reshape(PLANE, COL))
+    got = exchange(sent, ROWS1)
+    tend, sent, meta = physics(remap_cols, regime_row, got, tiles, hot, parts, remap_weights)
     back = exchange(sent, ROWS2)
     base = jnp.stack([device * 4, (device + 1 - 2 * core) * 4]).astype(jnp.int32)
     keep, send = ocean(base, meta, back)
     other = lax.ppermute(send, "dev", [(i, i ^ 1) for i in range(dev_count)])
-    new_mom = update(meta, back, mom)
+    new_mom = update(meta, back, mom_tiles)
     low = jnp.where(core == 0, keep, other).reshape(4, 2, LANES)
     high = jnp.where(core == 0, other, keep).reshape(4, 2, LANES)
     return (

time: 66 us -> 60 us (0.909)
  blocking collectives: 23.1 us -> 0 us
  starting transfers between devices: 6.01 us -> 17.5 us
  waiting for transfers between devices: 19.3 us -> 30 us
  Pallas kernels: 14.4 us -> 10.8 us
  local copies, waits for them, and re-layouts: 1.02 us -> 0.04 us
    all_to_all x1 -> x0, blocking collectives: 23.1 us -> none  [exchange(): lax.all_to_all(sent.reshape(PEERS, 1, rows * LANES), ('node', 'dev'), 0,...]
    all_to_all x1 -> x2, starting transfers between devices: 4.75 us -> 16.2 us  [exchange(): lax.all_to_all(sent.reshape(PEERS, 1, rows * LANES), ('node', 'dev'), 0,...]
    all_to_all x1 -> x2, waiting for transfers between devices: 19.3 us -> 30 us  [exchange(): lax.all_to_all(sent.reshape(PEERS, 1, rows * LANES), ('node', 'dev'), 0,...]
    pallas_call x4 -> x5, Pallas kernels: 14.4 us -> 10.8 us  [the longest x1 5.17 us: physics(): call(physics_kernel, [SMEM] + [VMEM] * 5 + [HBM], [far((PLANE, COL)), her...]
    unnamed x4 -> x6, local copies, waits for them, and re-layouts: 0.99 us -> 0.01 us
  transfers between devices with their start and end apart: 2 -> 3, of which waited for: 1 -> 2; matrix products, arithmetic and copies ran while one was open for 1% -> 0% of each run, Pallas kernels for 6% -> 4%
where the time goes in v1:
time: 60 us; the launch traced here: 59.7 us
  waiting for transfers between devices  30 us (50%)
  starting transfers between devices  17.5 us (29%)
  Pallas kernels  10.8 us (18%)
  between operations  0.75 us (1%)
  other arithmetic  0.69 us (1%)
    all_to_all x2, waiting for transfers between devices, exchange(): lax.all_to_all(sent.reshape(PEERS, 1, rows * LANES), ('node', 'dev'), 0,...  30 us
    all_to_all x2, starting transfers between devices, exchange(): lax.all_to_all(sent.reshape(PEERS, 1, rows * LANES), ('node', 'dev'), 0,...  16.2 us
    pallas_call x1, Pallas kernels, physics(): call(physics_kernel, [SMEM] + [VMEM] * 5 + [HBM], [far((PLANE, COL)), her...  5.17 us
    pallas_call x1, Pallas kernels, pack(): call(pack_kernel, [HBM] * 3, [here((ROWS1 * PEERS, LANES)), here((CAP, PL...  2.22 us
    pallas_call x1, Pallas kernels, update(): call(update_kernel, [VMEM] * 3, [far((PLANE, SLOTS))], [ANY], [pltpu.VMEM...  1.32 us
    pallas_call x1, Pallas kernels, prepare(): call(prepare_kernel, [VMEM, VMEM, HBM], [here((2, PLANE, LANES)), here((S...  1.27 us
    ppermute x1, starting transfers between devices, local(): other = lax.ppermute(send, 'dev', [(i, i ^ 1) for i in range(dev_count)])  1.26 us
  transfers between devices with their start and end apart: 3, of which 2 were waited for; matrix products, arithmetic and copies ran while one was open for 0% of the time, Pallas kernels for 4%

profile of v1, /device:TPU:1, one launch (start us, length us, event | category | flops | bytes accessed | tf_op | source)
XLA Modules:
  0.0 59.7 jit_solution(9553925870194327077)
XLA Ops:
  0.6 0.0 copy-start
  0.6 0.0 copy-start.1
  0.7 0.0 copy-start.2
  0.7 2.2 %pack.1 = (f32[640,128]{1,0:T(8,128)}, f32[4,576,128]{2,1,0:T(8,128)S(1)}) custom-call(s32[4]{0:T(128)} %rows_hbm.1, s32[1,256]{1,0:T(1,128)} %bitcast.15, f32[576,512]{1,0:T(8,128)} %bitcast.19), custom_call_target="tpu_custom_call" | custom-call | tf_op jit(solution)/shard_map/pack/pallas_call | solution.py:482
  2.9 11.5 %all-to-all-start = ((f32[128,1,640]{2,1,0:T(1,128)}), f32[128,1,640]{2,1,0:T(1,128)S(1)}, u32[]{:S(2)}, u32[]{:S(2)}) async-start(f32[128,1,640]{2,1,0:T(1,128)} %bitcast.3), calls=%async_computation | async-start | bytes 655360 | tf_op jit(solution)/shard_map/all_to_all | solution.py:558
  14.4 0.0 copy-done
  14.4 0.0 copy-done.1
  14.4 1.3 %prepare.1 = (f32[2,576,128]{2,1,0:T(8,128)S(1)}, bf16[512,256]{1,0:T(8,128)(2,1)S(1)}, f32[2,7,72,128]{3,2,1,0:T(8,128)S(1)}) custom-call(s32[1,256]{1,0:T(1,128)S(1)} %bitcast.16, s32[1,256]{1,0:T(1,128)S(1)} %bitcast.17, f32[576,256]{1,0:T(8,128)} %bitcast.21), custom_call_target="tpu_custom_call" | custom-call | tf_op jit(solution)/shard_map/prepare/pallas_call | solution.py:499
  15.7 10.2 %all-to-all-done = f32[128,1,640]{2,1,0:T(1,128)S(1)} async-done(((f32[128,1,640]{2,1,0:T(1,128)}), f32[128,1,640]{2,1,0:T(1,128)S(1)}, u32[]{:S(2)}, u32[]{:S(2)}) %all-to-all-start) | async-done | bytes 327712 | tf_op jit(solution)/shard_map/all_to_all | solution.py:558
  25.8 0.0 copy-done.2
  25.8 5.2 %physics.1 = (f32[576,256]{1,0:T(8,128)}, f32[2176,128]{1,0:T(8,128)}, f32[8,128]{1,0:T(8,128)S(1)}) custom-call(s32[4]{0:T(128)S(1)} %copy-done.2, s32[1,256]{1,0:T(1,128)S(1)} %bitcast.18, f32[640,128]{1,0:T(8,128)S(1)} %bitcast.14, f32[2,576,128]{2,1,0:T(8,128)S(1)} %get-tuple-element.14.tile_ref, bf16[512,256]{1,0:T(8,128)(2,1)S(1)} %get-tuple-element.15.hot_ref, ...), custom_call_target="tpu_custom_call" | custom-call | tf_op jit(solution)/shard_map/physics/pallas_call | solution.py:514
  31.0 4.8 %all-to-all-start.1 = ((f32[128,1,2176]{2,1,0:T(1,128)}), f32[128,1,2176]{2,1,0:T(1,128)S(1)}, u32[]{:S(2)}, u32[]{:S(2)}) async-start(f32[128,1,2176]{2,1,0:T(1,128)} %bitcast.7), calls=%async_computation.1 | async-start | bytes 2228224 | tf_op jit(solution)/shard_map/all_to_all | solution.py:558
  35.8 0.1 pad_add_fusion.base_ref
  35.9 19.8 %all-to-all-done.1 = f32[128,1,2176]{2,1,0:T(1,128)S(1)} async-done(((f32[128,1,2176]{2,1,0:T(1,128)}), f32[128,1,2176]{2,1,0:T(1,128)S(1)}, u32[]{:S(2)}, u32[]{:S(2)}) %all-to-all-start.1) | async-done | bytes 1114144 | tf_op jit(solution)/shard_map/all_to_all | solution.py:558
  55.7 0.8 %ocean.1 = (f32[4,256]{1,0:T(4,128)S(1)}, f32[4,256]{1,0:T(4,128)S(1)}) custom-call(s32[2]{0:T(128)S(1)} %pad_add_fusion.base_ref, f32[8,128]{1,0:T(8,128)S(1)} %get-tuple-element.18.meta_ref, f32[2176,128]{1,0:T(8,128)S(1)} %bitcast.12), custom_call_target="tpu_custom_call" | custom-call | tf_op jit(solution)/shard_map/ocean/pallas_call | solution.py:537
  56.5 1.3 %collective-permute-start = (f32[4,256]{1,0:T(4,128)S(1)}, f32[4,256]{1,0:T(4,128)S(1)}, u32[]{:S(2)}, u32[]{:S(2)}) collective-permute-start(f32[4,256]{1,0:T(4,128)S(1)} %get-tuple-element.22), channel_id=1, source_target_pairs={{0,1},{1,0},{2,3},{3,2},{4,5},{5,4},{6,7},{7,6},{8,9},{9,8},{10,11... | collective-permute-start | bytes 12296 | tf_op jit(solution)/shard_map/ppermute | solution.py:577
  57.7 1.3 %update.1 = f32[576,512]{1,0:T(8,128)} custom-call(f32[8,128]{1,0:T(8,128)S(1)} %get-tuple-element.18.meta_ref, f32[2176,128]{1,0:T(8,128)S(1)} %bitcast.13, f32[4,576,128]{2,1,0:T(8,128)S(1)} %get-tuple-element.20.tile_ref), custom_call_target="tpu_custom_call" | custom-call | tf_op jit(solution)/shard_map/update/pallas_call | solution.py:543
  59.1 0.0 collective-permute-done
  59.1 0.6 %pad_maximum_fusion = f32[4,4,128]{2,1,0:T(4,128)} fusion(f32[4,2,128]{2,1,0:T(2,128)S(1)} %reshape.53, f32[4,2,128]{2,1,0:T(2,128)S(1)} %reshape.52), kind=kLoop, calls=%fused_computation | loop fusion | flops 2048 | bytes 16384 | tf_op jit(solution)/shard_map/concatenate | solution.py:584
  (3 shorter events, 0.0 us)
Async XLA Ops:
  0.6 13.8 %copy-start = (s32[256,1]{0,1:T(1,128)S(1)}, s32[256,1]{0,1:T(1,128)}, u32[]{:S(2)}) copy-start(s32[256,1]{0,1:T(1,128)} %param.8) | copy-start | bytes 3076
  0.6 13.8 %copy-start.1 = (s32[256]{0:T(256)S(1)}, s32[256]{0:T(256)}, u32[]{:S(2)}) copy-start(s32[256]{0:T(256)} %param.9) | copy-start | bytes 3076
  0.7 25.2 %copy-start.2 = (s32[4]{0:T(128)S(1)}, s32[4]{0:T(128)}, u32[]{:S(2)}) copy-start(s32[4]{0:T(128)} %cols_ref.1) | copy-start | bytes 52
  2.9 23.0 %all-to-all-start = ((f32[128,1,640]{2,1,0:T(1,128)}), f32[128,1,640]{2,1,0:T(1,128)S(1)}, u32[]{:S(2)}, u32[]{:S(2)}) async-start(f32[128,1,640]{2,1,0:T(1,128)} %bitcast.3), calls=%async_computation | async-start | bytes 655360 | tf_op jit(solution)/shard_map/all_to_all | solution.py:558
  31.0 24.7 %all-to-all-start.1 = ((f32[128,1,2176]{2,1,0:T(1,128)}), f32[128,1,2176]{2,1,0:T(1,128)S(1)}, u32[]{:S(2)}, u32[]{:S(2)}) async-start(f32[128,1,2176]{2,1,0:T(1,128)} %bitcast.7), calls=%async_computation.1 | async-start | bytes 2228224 | tf_op jit(solution)/shard_map/all_to_all | solution.py:558
  56.5 2.6 %collective-permute-start = (f32[4,256]{1,0:T(4,128)S(1)}, f32[4,256]{1,0:T(4,128)S(1)}, u32[]{:S(2)}, u32[]{:S(2)}) collective-permute-start(f32[4,256]{1,0:T(4,128)S(1)} %get-tuple-element.22), channel_id=1, source_target_pairs={{0,1},{1,0},{2,3},{3,2},{4,5},{5,4},{6,7},{7,6},{8,9},{9,8},{10,11... | collective-permute-start | bytes 12296 | tf_op jit(solution)/shard_map/ppermute | solution.py:577

commit v2 on v1

--- a/solution.py
+++ b/solution.py
@@ -47,21 +47,23 @@
 
 
 def pack_kernel(
-    rows_hbm, owner_hbm, mom_ref, out_ref, tile_ref, rows_ref, owner_ref, block_ref, sem, small_sem
+    rows_hbm, owner_hbm, mom_ref, out_ref, rows_ref, owner_ref, block_ref, sem, small_sem
 ):
     small = [
         pltpu.make_async_copy(owner_hbm, owner_ref, small_sem.at[0]),
         pltpu.make_async_copy(rows_hbm, rows_ref, small_sem.at[1]),
     ]
-    for copy in small:
-        copy.start()
-    copies = [
-        pltpu.make_async_copy(
-            mom_ref.at[:, pl.ds(p * LANES, LANES)], tile_ref.at[p], sem.at[p]
-        )
-        for p in range(CAP)
-    ]
-    for copy in copies:
+    copies = []
+    for p in range(CAP):
+        for at, moment in enumerate((0, 2)):
+            copies.append(
+                pltpu.make_async_copy(
+                    mom_ref.at[:, moment, pl.ds(p * LANES, LANES)],
+                    block_ref.at[pl.ds((p * DOWN + at) * LEV, LEV), :],
+                    sem.at[p, at],
+                )
+            )
+    for copy in small + copies:
         copy.start()
     for copy in small:
         copy.wait()
@@ -74,11 +76,8 @@
     for n in range(4):
         meta = jnp.where(which == n, rows_ref[n].astype(f32), meta)
     block_ref[META:, :] = meta
-    for p in range(CAP):
-        copies[p].wait()
-        for at, moment in enumerate((0, 2)):
-            first = (p * DOWN + at) * LEV
-            block_ref[first : first + LEV, :] = tile_ref[p, pl.ds(moment, LEV, stride=FLD), :]
+    for copy in copies:
+        copy.wait()
     for t in range(ROWS1):
         out_ref[pl.ds(t, PEERS, stride=ROWS1), :] = block_ref[t * LANES : (t + 1) * LANES, :].T
 
@@ -135,38 +134,41 @@
     )
 
 
-def solve(a_ref, k_ref, y_ref, g_ref):
+def solve(a_ref, k_ref, c_ref, y_ref, g_ref):
     halves = range(COL // LANES)
 
-    def kap(h, level):
-        row = k_ref[level : level + 1, h * LANES : (h + 1) * LANES]
-        return jnp.broadcast_to(row, (FLD, LANES))
+    def row(ref, h, level):
+        one = ref[level : level + 1, h * LANES : (h + 1) * LANES]
+        return jnp.broadcast_to(one, (FLD, LANES))
 
     def rows(h, level):
         first = h * PAD_ROWS + level * FLD
         return slice(first, first + FLD)
 
     state = {}
+    ends = {}
     for step in range(HALF):
         for h in halves:
             for chain in range(2):
                 k = LEV - 1 - step if chain else step
-                k_new = kap(h, k - 1 if chain else k)
+                k_new = row(k_ref, h, k - 1 if chain else k)
                 a = a_ref[rows(h, k), :]
                 if step == 0:
-                    r = 1.0 / (1.0 + k_new)
+                    r = 1.0 / row(c_ref, h, k)
                     d = a * r
                 else:
-                    k_old, g, d = state[h, chain]
-                    r = 1.0 / (1.0 + k_new + k_old * (1.0 - g))
-                    d = (a + k_old * d) * r
+                    k_old, r, d = state[h, chain]
+                    r = 1.0 / (row(c_ref, h, k) - (k_old * k_old) * r)
+                    d = a * r + (k_old * r) * d
                 g = k_new * r
                 g_ref[rows(h, k), :] = g
                 y_ref[rows(h, k), :] = d
-                state[h, chain] = (k_new, g, d)
+                state[h, chain] = (k_new, r, d)
+                ends[h, chain] = g
     z = {}
     for h in halves:
-        (_, g_up, d_up), (_, g_dn, d_dn) = state[h, 0], state[h, 1]
+        d_up, d_dn = state[h, 0][2], state[h, 1][2]
+        g_up, g_dn = ends[h, 0], ends[h, 1]
         z[h, 0] = (d_up + g_up * d_dn) / (1.0 - g_up * g_dn)
         z[h, 1] = d_dn + g_dn * z[h, 0]
         y_ref[rows(h, HALF - 1), :] = z[h, 0]
@@ -185,7 +187,9 @@
 
 
 def prepare_kernel(
-    owner_ref, regime_ref, state_ref, tile_ref, hot_ref, part_ref, sem
+    owner_ref, regime_ref, state_ref, mom_ref, weight_ref,
+    tile_ref, hot_ref, part_ref, mom_tile_ref, weight_part_ref,
+    weight_own, sem, mom_sem, weight_sem,
 ):
     copies = [
         pltpu.make_async_copy(
@@ -193,7 +197,14 @@
         )
         for h in range(COL // LANES)
     ]
-    for copy in copies:
+    weights = pltpu.make_async_copy(weight_ref, weight_own, weight_sem)
+    moments = [
+        pltpu.make_async_copy(
+            mom_ref.at[:, pl.ds(p * LANES, LANES)], mom_tile_ref.at[p], mom_sem.at[p]
+        )
+        for p in range(CAP)
+    ]
+    for copy in copies + [weights] + moments:
         copy.start()
     owner_row = owner_ref[...]
     owner_down = columns_down(owner_row)
@@ -220,20 +231,27 @@
             kept, source, excess, above = micro_free(x, warm, mixed, icy, above, top)
             for f, value in enumerate(kept + (source, excess)):
                 part_ref[h, f, i * 8 : i * 8 + 8, :] = value
+    weights.wait()
+    for n in range(4):
+        down, across = (n % 2) * LANES, (n // 2) * LANES
+        for at, part in enumerate(split3(weight_own[n])):
+            weight_part_ref[at, down : down + LANES, across : across + LANES] = part
+    for copy in moments:
+        copy.wait()
 
 
 def physics_kernel(
+    device_ref,
     cols_ref,
     regime_ref,
     got_ref,
     tile_ref,
     hot_ref,
     part_ref,
-    weight_hbm,
+    weight_ref,
     tend_out,
     out_ref,
     meta_ref,
-    weight_ref,
     tend_ref,
     block_ref,
     mom_ref,
@@ -241,15 +259,20 @@
     y_ref,
     g_ref,
     k_ref,
+    c_ref,
     e_ref,
-    weight_sem,
     tend_sem,
 ):
-    weights = pltpu.make_async_copy(weight_hbm, weight_ref, weight_sem)
-    weights.start()
     for t in range(ROWS1):
         block_ref[t * LANES : (t + 1) * LANES, :] = got_ref[pl.ds(t, PEERS, stride=ROWS1), :].T
-    meta_ref[...] = block_ref[META : META + 8, :]
+    device = device_ref[0]
+    core = device % 2
+    meta_ref[0:2, :] = jnp.where(
+        core == 1, block_ref[META + 2 : META + 4, :], block_ref[META : META + 2, :]
+    )
+    meta_ref[2:3, :] = jnp.full((1, PEERS), (device * 4).astype(f32))
+    meta_ref[3:4, :] = jnp.full((1, PEERS), ((device + 1 - 2 * core) * 4).astype(f32))
+    meta_ref[4:8, :] = block_ref[META + 4 : META + 8, :]
     slotted = jnp.concatenate(
         [block_ref[p * DOWN * LEV : (p + 1) * DOWN * LEV, :] for p in range(CAP)], axis=1
     )
@@ -291,6 +314,7 @@
         src = a_ref if turn == 0 else y_ref
         for h in range(COL // LANES):
             lanes = slice(h * LANES, (h + 1) * LANES)
+            above = jnp.zeros((8, LANES), f32)
             for i in range(LEV // 8):
 
                 def drop(f):
@@ -303,11 +327,60 @@
                 du, dv, dt = drop(5), drop(6), drop(0)
                 shear = du * du + dv * dv
                 mixing = 0.3 + 1.5 * shear / (1.0 + shear) * (0.5 - 0.5 * jnp.tanh(dt))
-                k_ref[i * 8 : i * 8 + 8, lanes] = mixing * e_ref[i * 8 : i * 8 + 8, lanes]
-        solve(a_ref, k_ref, y_ref, g_ref)
+                kappa = mixing * e_ref[i * 8 : i * 8 + 8, lanes]
+                rolled = pltpu.roll(kappa, 1, 0)
+                k_ref[i * 8 : i * 8 + 8, lanes] = kappa
+                c_ref[i * 8 : i * 8 + 8, lanes] = 1.0 + kappa + jnp.where(top, above, rolled)
+                above = rolled
+        solve(a_ref, k_ref, c_ref, y_ref, g_ref)
 
     field = iota((FLD, LANES), 0)
     kept = (field >= 2) & (field <= 4)
+    bottom = []
+    for h in range(COL // LANES):
+        level = slice((LEV - 1) * FLD, LEV * FLD)
+        at = slice(h * PAD_ROWS + (LEV - 1) * FLD, h * PAD_ROWS + LEV * FLD)
+        old = tile_ref[h, level, :]
+        bottom.append(old + (jnp.where(kept, a_ref[at, :], y_ref[at, :]) - old))
+    b = jnp.concatenate(bottom, axis=1)
+    b0, b3, b5, b6 = (b[f : f + 1, :] for f in (0, 3, 5, 6))
+    wind = jnp.sqrt(1.0 + b5 * b5 + b6 * b6)
+    flux = jnp.concatenate(
+        [
+            -0.5 * wind * b5,
+            -0.5 * wind * b6,
+            0.5 * softplus(b3),
+            -0.3 * wind * b0,
+            jnp.zeros((4, COL), f32),
+        ],
+        axis=0,
+    )
+    none = jnp.zeros((FLD, LANES), f32)
+    used = []
+    for n in range(4):
+        mine = jnp.where(cols_ref[n] == 0, flux[:, :LANES], flux[:, LANES:])
+        used.append(jnp.concatenate([none, mine] if n % 2 else [mine, none], axis=1))
+    hi, mid, low = split3(jnp.concatenate(used, axis=0))
+
+    def weighted(parts, at):
+        got = jnp.dot(
+            jnp.concatenate(parts, axis=0), weight_ref[at], preferred_element_type=f32
+        )
+        total = got[0:32, :]
+        for i in range(1, len(parts)):
+            total = total + got[i * 32 : i * 32 + 32, :]
+        return total
+
+    products = weighted([hi], 2) + weighted([hi, mid], 1) + weighted([hi, mid, low], 0)
+    odd = iota((PEERS, LANES), 0) % 2 == 1
+    for n in range(2):
+        for e in range(4):
+            even_row = products[n * 8 + e : n * 8 + e + 1, 0:LANES]
+            odd_row = products[n * 8 + 16 + e : n * 8 + 17 + e, LANES:]
+            out_ref[pl.ds(ROWS_UP + 4 * n + e, PEERS, stride=ROWS2), :] = jnp.where(
+                odd, odd_row, even_row
+            )
+
     copies = []
     for h in range(COL // LANES):
         for k in range(LEV):
@@ -331,64 +404,45 @@
         ],
         axis=1,
     )
-    total = None
-    for part in split3(fields):
-        got = lax.dot_general(
-            part, hot_ref[...], (((1,), (1,)), ((), ())), preferred_element_type=f32
-        )
-        total = got if total is None else total + got
-    for p in range(CAP):
-        block_ref[p * UP * LEV : (p + 1) * UP * LEV, :] = total[:, p * PEERS : (p + 1) * PEERS]
-    for t in range(ROWS_UP):
-        out_ref[pl.ds(t, PEERS, stride=ROWS2), :] = block_ref[t * LANES : (t + 1) * LANES, :].T
-
-    bottom = slice((LEV - 1) * FLD, LEV * FLD)
-    b = jnp.concatenate(
-        [tile_ref[h, bottom, :] + tend_ref[h, bottom, :] for h in range(COL // LANES)], axis=1
-    )
-    b0, b3, b5, b6 = (b[f : f + 1, :] for f in (0, 3, 5, 6))
-    wind = jnp.sqrt(1.0 + b5 * b5 + b6 * b6)
-    flux = jnp.concatenate(
-        [
-            -0.5 * wind * b5,
-            -0.5 * wind * b6,
-            0.5 * softplus(b3),
-            -0.3 * wind * b0,
-            jnp.zeros((4, COL), f32),
-        ],
-        axis=0,
-    )
-    odd = iota((PEERS, LANES), 0) % 2 == 1
-    weights.wait()
-    for n in range(4):
-        used = jnp.where(cols_ref[n] == 0, flux[:, :LANES], flux[:, LANES:])
-        product = jnp.dot(
-            used, weight_ref[n], precision=lax.Precision.HIGHEST, preferred_element_type=f32
-        )
-        for e in range(2):
-            out_ref[pl.ds(ROWS_UP + 2 * n + e, PEERS, stride=ROWS2), :] = jnp.where(
-                odd, product[2 + e : 3 + e, :], product[e : e + 1, :]
-            )
+    parts = split3(fields)
+    sent = 0
+    for pair in range(CAP // 2):
+        hot = hot_ref[pair * 2 * PEERS : (pair + 1) * 2 * PEERS, :]
+        total = None
+        for part in parts:
+            got = lax.dot_general(
+                part, hot, (((1,), (1,)), ((), ())), preferred_element_type=f32
+            )
+            total = got if total is None else total + got
+        for q in range(2):
+            first = (pair * 2 + q) * UP * LEV
+            block_ref[first : first + UP * LEV, :] = total[:, q * PEERS : (q + 1) * PEERS]
+        ready = (pair + 1) * 2 * UP * LEV // LANES
+        for t in range(sent, ready):
+            out_ref[pl.ds(t, PEERS, stride=ROWS2), :] = block_ref[
+                t * LANES : (t + 1) * LANES, :
+            ].T
+        sent = ready
     for copy in copies:
         copy.wait()
 
 
-def ocean_kernel(base_ref, meta_ref, got_ref, keep_ref, send_ref):
-    row = iota((8, PEERS), 0)
-    wanted = jnp.where(row < 4, base_ref[0] + row, base_ref[1] + row - 4).astype(f32)
+def ocean_kernel(meta_ref, got_ref, keep_ref, send_ref):
+    row = iota((8, PEERS), 0).astype(f32)
+    wanted = jnp.where(row < 3.5, meta_ref[2:3, :] + row, meta_ref[3:4, :] + (row - 4.0))
     chosen = jnp.concatenate(
-        [(meta_ref[n : n + 1, :] == wanted).astype(bf16) for n in range(4)], axis=1
+        [(meta_ref[n : n + 1, :] == wanted).astype(bf16) for n in range(2)], axis=1
     )
     values = jnp.concatenate(
         [
             jnp.concatenate(
                 [
-                    got_ref[pl.ds(ROWS_UP + 2 * n + e, PEERS, stride=ROWS2), :]
-                    for e in range(2)
+                    got_ref[pl.ds(ROWS_UP + 4 * n + e, PEERS, stride=ROWS2), :]
+                    for e in range(4)
                 ],
                 axis=1,
             )
-            for n in range(4)
+            for n in range(2)
         ],
         axis=0,
     )
@@ -396,8 +450,10 @@
     for part in split3(values):
         got = jnp.dot(chosen, part, preferred_element_type=f32)
         total = got if total is None else total + got
-    keep_ref[...] = total[0:4, :]
-    send_ref[...] = total[4:8, :]
+    for e in range(4):
+        part = total[:, e * LANES : (e + 1) * LANES]
+        keep_ref[:, e, :] = part[0:4, :]
+        send_ref[:, e, :] = part[4:8, :]
 
 
 def update_kernel(meta_ref, got_ref, tile_ref, out_ref, block_ref, new_ref, sem):
@@ -482,42 +538,48 @@
     return call(
         pack_kernel,
         [HBM] * 3,
-        [here((ROWS1 * PEERS, LANES)), here((CAP, PLANE, LANES))],
-        [VMEM] * 2,
+        [here((ROWS1 * PEERS, LANES))],
+        [VMEM],
         [
             pltpu.SMEM((4,), jnp.int32),
             pltpu.VMEM((1, COL), jnp.int32),
             pltpu.VMEM((ROWS1 * LANES, LANES), f32),
-            pltpu.SemaphoreType.DMA((CAP,)),
+            pltpu.SemaphoreType.DMA((CAP, DOWN)),
             pltpu.SemaphoreType.DMA((2,)),
         ],
         "pack",
-    )(outside(rows), outside(owner_row), outside(mom))
-
-
-def prepare(owner_row, regime_row, state):
+    )(outside(rows), outside(owner_row), outside(mom))[0]
+
+
+def prepare(owner_row, regime_row, state, mom, weights):
     return call(
         prepare_kernel,
-        [VMEM, VMEM, HBM],
+        [VMEM] * 2 + [HBM] * 3,
         [
             here((2, PLANE, LANES)),
             here((SLOTS, COL), bf16),
             here((2, 7, LEV, LANES)),
-        ],
-        [VMEM] * 3,
-        [pltpu.SemaphoreType.DMA((2,))],
+            here((CAP, PLANE, LANES)),
+            here((3, 2 * LANES, 2 * LANES), bf16),
+        ],
+        [VMEM] * 5,
+        [
+            pltpu.VMEM((4, LANES, LANES), f32),
+            pltpu.SemaphoreType.DMA((2,)),
+            pltpu.SemaphoreType.DMA((CAP,)),
+            pltpu.SemaphoreType.DMA,
+        ],
         "prepare",
-    )(owner_row, regime_row, outside(state))
-
-
-def physics(cols, regime_row, got, tiles, hot, parts, weights):
+    )(owner_row, regime_row, outside(state), outside(mom), outside(weights))
+
+
+def physics(device, cols, regime_row, got, tiles, hot, parts, weights):
     return call(
         physics_kernel,
-        [SMEM] + [VMEM] * 5 + [HBM],
+        [SMEM] * 2 + [VMEM] * 6,
         [far((PLANE, COL)), here((ROWS2 * PEERS, LANES)), here((8, PEERS))],
         [ANY, VMEM, VMEM],
         [
-            pltpu.VMEM((4, LANES, LANES), f32),
             pltpu.VMEM((2, PLANE, LANES), f32),
             pltpu.VMEM((ROWS_UP * LANES, LANES), f32),
             pltpu.VMEM((DOWN * LEV + 8, COL), f32),
@@ -526,17 +588,17 @@
             pltpu.VMEM((2 * PAD_ROWS, LANES), f32),
             pltpu.VMEM((LEV, COL), f32),
             pltpu.VMEM((LEV, COL), f32),
-            pltpu.SemaphoreType.DMA,
+            pltpu.VMEM((LEV, COL), f32),
             pltpu.SemaphoreType.DMA((2,)),
         ],
         "physics",
-    )(cols, regime_row, *(hold(x) for x in (got, tiles, hot, parts)), outside(weights))
-
-
-def ocean(base, meta, back):
+    )(device, cols, regime_row, *(hold(x) for x in (got, tiles, hot, parts, weights)))
+
+
+def ocean(meta, back):
     return call(
-        ocean_kernel, [SMEM, VMEM, VMEM], [here((4, 2 * LANES))] * 2, [VMEM] * 2, [], "ocean"
-    )(base, hold(meta), hold(back))
+        ocean_kernel, [VMEM, VMEM], [here((4, 4, LANES))] * 2, [VMEM] * 2, [], "ocean"
+    )(hold(meta), hold(back))
 
 
 def update(meta, back, tiles):
@@ -563,26 +625,24 @@
 
 def local(state, span_owner, regime, moments, remap_weights, remap_rows, remap_cols):
     dev_count = lax.axis_size("dev")
-    core = lax.axis_index("dev") % 2
-    device = lax.axis_index(("node", "dev"))
+    device = lax.axis_index(("node", "dev")).astype(jnp.int32).reshape(1)
     owner_row = span_owner.reshape(1, COL)
     regime_row = regime.reshape(1, COL)
-    sent, mom_tiles = pack(remap_rows, owner_row, moments.reshape(PLANE, SLOTS))
-    tiles, hot, parts = prepare(owner_row, regime_row, state.reshape(PLANE, COL))
+    sent = pack(remap_rows, owner_row, moments)
+    tiles, hot, parts, mom_tiles, weights = prepare(
+        owner_row,
+        regime_row,
+        state.reshape(PLANE, COL),
+        moments.reshape(PLANE, SLOTS),
+        remap_weights,
+    )
     got = exchange(sent, ROWS1)
-    tend, sent, meta = physics(remap_cols, regime_row, got, tiles, hot, parts, remap_weights)
+    tend, sent, meta = physics(device, remap_cols, regime_row, got, tiles, hot, parts, weights)
     back = exchange(sent, ROWS2)
-    base = jnp.stack([device * 4, (device + 1 - 2 * core) * 4]).astype(jnp.int32)
-    keep, send = ocean(base, meta, back)
+    keep, send = ocean(meta, back)
     other = lax.ppermute(send, "dev", [(i, i ^ 1) for i in range(dev_count)])
     new_mom = update(meta, back, mom_tiles)
-    low = jnp.where(core == 0, keep, other).reshape(4, 2, LANES)
-    high = jnp.where(core == 0, other, keep).reshape(4, 2, LANES)
-    return (
-        tend.reshape(LEV, FLD, COL),
-        new_mom.reshape(LEV, FLD, SLOTS),
-        jnp.concatenate([low, high], axis=1),
-    )
+    return tend.reshape(LEV, FLD, COL), new_mom.reshape(LEV, FLD, SLOTS), keep + other
 
 
 def solution(mesh):

time: 60 us -> 57.6 us (0.960)
  blocking collectives: 0 us -> 24.4 us
  waiting for transfers between devices: 30 us -> 9.79 us
  starting transfers between devices: 17.5 us -> 12.8 us
  Pallas kernels: 10.8 us -> 8.98 us
    all_to_all x0 -> x1, blocking collectives: none -> 24.4 us  [exchange(): lax.all_to_all(sent.reshape(PEERS, 1, rows * LANES), ('node', 'dev'), 0,...]
    all_to_all x2 -> x1, waiting for transfers between devices: 30 us -> 9.78 us  [exchange(): lax.all_to_all(sent.reshape(PEERS, 1, rows * LANES), ('node', 'dev'), 0,...]
    all_to_all x2 -> x1, starting transfers between devices: 16.2 us -> 11.5 us  [exchange(): lax.all_to_all(sent.reshape(PEERS, 1, rows * LANES), ('node', 'dev'), 0,...]
    pallas_call x4, Pallas kernels: 9.43 us -> 7.65 us  [the longest x1 3.81 us: physics(): call(physics_kernel, [SMEM] * 2 + [VMEM] * 6, [far((PLANE, COL)), here((R...]
    concatenate x1 -> x0, other arithmetic: 0.61 us -> none  [local(): jnp.concatenate([low, high], axis=1)]
    add x0 -> x1, other arithmetic: none -> 0.6 us  [local(): keep + other]
  transfers between devices with their start and end apart: 3 -> 2, of which waited for: 2 -> 1; matrix products, arithmetic and copies ran while one was open for 0% -> 0% of each run, Pallas kernels for 4% -> 5%
where the time goes in v2:
time: 57.6 us; the launch traced here: 57.4 us
  blocking collectives  24.4 us (42%)
  starting transfers between devices  12.8 us (22%)
  waiting for transfers between devices  9.79 us (17%)
  Pallas kernels  8.98 us (16%)
  between operations  0.73 us (1%)
  other arithmetic  0.6 us (1%)
    all_to_all x1, blocking collectives, exchange(): lax.all_to_all(sent.reshape(PEERS, 1, rows * LANES), ('node', 'dev'), 0,...  24.4 us
    all_to_all x1, starting transfers between devices, exchange(): lax.all_to_all(sent.reshape(PEERS, 1, rows * LANES), ('node', 'dev'), 0,...  11.5 us
    all_to_all x1, waiting for transfers between devices, exchange(): lax.all_to_all(sent.reshape(PEERS, 1, rows * LANES), ('node', 'dev'), 0,...  9.78 us
    pallas_call x1, Pallas kernels, physics(): call(physics_kernel, [SMEM] * 2 + [VMEM] * 6, [far((PLANE, COL)), here((R...  3.81 us
    pallas_call x1, Pallas kernels, pack(): call(pack_kernel, [HBM] * 3, [here((ROWS1 * PEERS, LANES))], [VMEM], [plt...  1.95 us
    pallas_call x1, Pallas kernels, prepare(): call(prepare_kernel, [VMEM] * 2 + [HBM] * 3, [here((2, PLANE, LANES)), he...  1.62 us
    ppermute x1, starting transfers between devices, local(): other = lax.ppermute(send, 'dev', [(i, i ^ 1) for i in range(dev_count)])  1.34 us
    pallas_call x1, Pallas kernels, update(): call(update_kernel, [VMEM] * 3, [far((PLANE, SLOTS))], [ANY], [pltpu.VMEM...  1.33 us
  transfers between devices with their start and end apart: 2, of which 1 were waited for; matrix products, arithmetic and copies ran while one was open for 0% of the time, Pallas kernels for 5%

profile of v2, /device:TPU:1, one launch (start us, length us, event | category | flops | bytes accessed | tf_op | source)
XLA Modules:
  0.0 57.4 jit_solution(2027717949586748674)
XLA Ops:
  0.6 0.0 copy-start.1
  0.6 0.0 copy-start
  0.7 2.0 %pack.1 = f32[640,128]{1,0:T(8,128)} custom-call(s32[4]{0:T(128)} %rows_hbm.1, s32[1,256]{1,0:T(1,128)} %bitcast.17, f32[72,8,512]{2,1,0:T(8,128)} %mom_ref.1), custom_call_target="tpu_custom_call" | custom-call | tf_op jit(solution)/shard_map/pack/pallas_call | solution.py:538
  2.6 11.5 %all-to-all-start = ((f32[128,1,640]{2,1,0:T(1,128)}), f32[128,1,640]{2,1,0:T(1,128)S(1)}, u32[]{:S(2)}, u32[]{:S(2)}) async-start(f32[128,1,640]{2,1,0:T(1,128)} %bitcast.3), calls=%async_computation | async-start | bytes 655360 | tf_op jit(solution)/shard_map/all_to_all | solution.py:620
  14.1 0.0 copy-start.2
  14.1 0.0 copy-done.1
  14.1 0.0 copy-done
  14.1 1.6 %prepare.1 = (f32[2,576,128]{2,1,0:T(8,128)S(1)}, bf16[512,256]{1,0:T(8,128)(2,1)S(1)}, f32[2,7,72,128]{3,2,1,0:T(8,128)S(1)}, f32[4,576,128]{2,1,0:T(8,128)S(1)}, bf16[3,256,256]{2,1,0:T(8,128)(2,1)S(1)}) custom-call(s32[1,256]{1,0:T(1,128)S(1)} %bitcast.18, s32[1,256]{1,0:T(1,128)S(1)} %bitcast.15, f32[576,256]{1,0:T(8,128)} %bitcast.21, ...), custom_call_target="tpu_custom_call" | custom-call | tf_op jit(solution)/shard_map/prepare/pallas_call | solution.py:555
  15.8 9.8 %all-to-all-done = f32[128,1,640]{2,1,0:T(1,128)S(1)} async-done(((f32[128,1,640]{2,1,0:T(1,128)}), f32[128,1,640]{2,1,0:T(1,128)S(1)}, u32[]{:S(2)}, u32[]{:S(2)}) %all-to-all-start) | async-done | bytes 327712 | tf_op jit(solution)/shard_map/all_to_all | solution.py:620
  25.6 0.0 copy-done.2
  25.6 3.8 %physics.1 = (f32[576,256]{1,0:T(8,128)}, f32[2176,128]{1,0:T(8,128)S(1)}, f32[8,128]{1,0:T(8,128)S(1)}) custom-call(s32[1]{0:T(128)} %bitcast.device_ref, s32[4]{0:T(128)S(1)} %copy-done.2, s32[1,256]{1,0:T(1,128)S(1)} %bitcast.16, f32[640,128]{1,0:T(8,128)S(1)} %bitcast.13, f32[2,576,128]{2,1,0:T(8,128)S(1)} %get-tuple-element.13.tile_ref, ...), custom_call_target="tpu_custom_call" | custom-call | tf_op jit(solution)/shard_map/physics/pallas_call | solution.py:577
  29.4 24.4 %all_to_all.10 = f32[128,1,2176]{2,1,0:T(1,128)S(1)} all-to-all(f32[128,1,2176]{2,1,0:T(1,128)S(1)} %bitcast.14), channel_id=1, replica_groups=mesh['node'=4,'dev'=32] {'node','dev'}, dimensions={0} | all-to-all | bytes 2228224 | tf_op jit(solution)/shard_map/all_to_all | solution.py:620
  53.8 0.3 ocean.1
  54.1 1.3 %collective-permute-start = (f32[4,4,128]{2,1,0:T(4,128)S(1)}, f32[4,4,128]{2,1,0:T(4,128)S(1)}, u32[]{:S(2)}, u32[]{:S(2)}) collective-permute-start(f32[4,4,128]{2,1,0:T(4,128)S(1)} %get-tuple-element.22), channel_id=1, source_target_pairs={{0,1},{1,0},{2,3},{3,2},{4,5},{5,4},{6,7},{7,6},{8,9},{9,8},{10,11... | collective-permute-start | bytes 24584 | tf_op jit(solution)/shard_map/ppermute | solution.py:643
  55.4 1.3 %update.1 = f32[576,512]{1,0:T(8,128)} custom-call(f32[8,128]{1,0:T(8,128)S(1)} %get-tuple-element.18.meta_ref, f32[2176,128]{1,0:T(8,128)S(1)} %bitcast.12, f32[4,576,128]{2,1,0:T(8,128)S(1)} %get-tuple-element.20.tile_ref), custom_call_target="tpu_custom_call" | custom-call | tf_op jit(solution)/shard_map/update/pallas_call | solution.py:605
  56.7 0.0 collective-permute-done
  56.8 0.6 %add.7 = f32[4,4,128]{2,1,0:T(4,128)} add(f32[4,4,128]{2,1,0:T(4,128)S(1)} %get-tuple-element.21, f32[4,4,128]{2,1,0:T(4,128)S(1)} %collective-permute-done) | non-fusion elementwise | flops 2048 | bytes 24576 | tf_op jit(solution)/shard_map/add | solution.py:645
Async XLA Ops:
  0.6 13.5 %copy-start.1 = (s32[256,1]{0,1:T(1,128)S(1)}, s32[256,1]{0,1:T(1,128)}, u32[]{:S(2)}) copy-start(s32[256,1]{0,1:T(1,128)} %param.8) | copy-start | bytes 3076
  0.6 13.5 %copy-start = (s32[256]{0:T(256)S(1)}, s32[256]{0:T(256)}, u32[]{:S(2)}) copy-start(s32[256]{0:T(256)} %param.9) | copy-start | bytes 3076
  2.6 23.0 %all-to-all-start = ((f32[128,1,640]{2,1,0:T(1,128)}), f32[128,1,640]{2,1,0:T(1,128)S(1)}, u32[]{:S(2)}, u32[]{:S(2)}) async-start(f32[128,1,640]{2,1,0:T(1,128)} %bitcast.3), calls=%async_computation | async-start | bytes 655360 | tf_op jit(solution)/shard_map/all_to_all | solution.py:620
  14.1 11.5 %copy-start.2 = (s32[4]{0:T(128)S(1)}, s32[4]{0:T(128)}, u32[]{:S(2)}) copy-start(s32[4]{0:T(128)} %cols_ref.1) | copy-start | bytes 52
  54.1 2.7 %collective-permute-start = (f32[4,4,128]{2,1,0:T(4,128)S(1)}, f32[4,4,128]{2,1,0:T(4,128)S(1)}, u32[]{:S(2)}, u32[]{:S(2)}) collective-permute-start(f32[4,4,128]{2,1,0:T(4,128)S(1)} %get-tuple-element.22), channel_id=1, source_target_pairs={{0,1},{1,0},{2,3},{3,2},{4,5},{5,4},{6,7},{7,6},{8,9},{9,8},{10,11... | collective-permute-start | bytes 24584 | tf_op jit(solution)/shard_map/ppermute | solution.py:643

commit v3 on v2

--- a/solution.py
+++ b/solution.py
@@ -21,6 +21,7 @@
 ROWS2 = ROWS_UP + OCN_ROWS
 HALF = LEV // 2
 PAD_ROWS = LEV * FLD + FLD
+PARTS = 9
 f32 = jnp.float32
 bf16 = jnp.bfloat16
 
@@ -29,12 +30,9 @@
     return lax.broadcasted_iota(jnp.int32, shape, axis)
 
 
-def split3(x):
+def split2(x):
     hi = x.astype(bf16)
-    rest = x - hi.astype(f32)
-    mid = rest.astype(bf16)
-    low = (rest - mid.astype(f32)).astype(bf16)
-    return hi, mid, low
+    return hi, (x - hi.astype(f32)).astype(bf16)
 
 
 def columns_down(owner_row):
@@ -86,11 +84,17 @@
     return jnp.maximum(x, 0.0) + jnp.log(1.0 + jnp.exp(-jnp.abs(x)))
 
 
-def micro_free(x, warm, mixed, icy, above, top):
+def rain_fall(rain, above, top):
+    rain_q = softplus(rain)
+    falling = 0.5 * rain_q
+    rolled = pltpu.roll(falling, 1, 0)
+    return rain_q, rain + 0.5 * (jnp.where(top, above, rolled) - falling), rolled
+
+
+def micro_free(x, rain_q, warm, mixed, icy):
     temper, vap, liq, rain, ice = x
     vapour = softplus(vap)
     liquid = softplus(liq)
-    rain_q = softplus(rain)
     ice_q = softplus(ice)
     half_t = jnp.tanh(0.5 * temper)
     satur = 0.6 * jnp.exp(0.5 * half_t)
@@ -100,9 +104,6 @@
     freeze = 0.3 * liquid * (0.5 - 0.5 * half_t)
     melting = 0.2 * ice_q * (0.5 + 0.5 * half_t)
     aggreg = 0.25 * ice_q * ice_q / (1.0 + ice_q)
-    falling = 0.5 * rain_q
-    rolled = pltpu.roll(falling, 1, 0)
-    from_above = jnp.where(top, above, rolled)
     source = jnp.where(
         icy, 0.175 * jnp.tanh(vapour - 0.8 * satur), 0.2 * jnp.tanh(excess)
     )
@@ -115,11 +116,10 @@
         temper + pick(-0.4 * evapor, 0.25 * swap, 0.25 * freeze),
         jnp.where(warm, vap + 0.5 * evapor, vap),
         liq - 0.5 * pick(autoconv, freeze + autoconv, freeze),
-        rain
-        + 0.5 * (pick(autoconv - evapor, autoconv + melting, aggreg) + from_above - falling),
+        rain + 0.5 * pick(autoconv - evapor, autoconv + melting, aggreg),
         jnp.where(warm, ice, ice + 0.5 * jnp.where(mixed, swap, freeze - aggreg)),
     )
-    return kept, source, excess, rolled
+    return kept, source, excess
 
 
 def micro_bound(kept, source, excess, m2, icy):
@@ -145,30 +145,43 @@
         first = h * PAD_ROWS + level * FLD
         return slice(first, first + FLD)
 
-    state = {}
-    ends = {}
-    for step in range(HALF):
-        for h in halves:
-            for chain in range(2):
-                k = LEV - 1 - step if chain else step
-                k_new = row(k_ref, h, k - 1 if chain else k)
-                a = a_ref[rows(h, k), :]
-                if step == 0:
-                    r = 1.0 / row(c_ref, h, k)
-                    d = a * r
-                else:
-                    k_old, r, d = state[h, chain]
-                    r = 1.0 / (row(c_ref, h, k) - (k_old * k_old) * r)
-                    d = a * r + (k_old * r) * d
-                g = k_new * r
-                g_ref[rows(h, k), :] = g
-                y_ref[rows(h, k), :] = d
-                state[h, chain] = (k_new, r, d)
-                ends[h, chain] = g
+    def base(h, chain, step):
+        return row(c_ref, h, LEV - 1 - step if chain else step)
+
+    def link(h, chain, step):
+        return row(k_ref, h, LEV - 1 - step if chain else step - 1)
+
+    def finish(h, chain, step, r):
+        k = LEV - 1 - step if chain else step
+        d = a_ref[rows(h, k), :] * r
+        if step > 0:
+            d = d + (link(h, chain, step) * r) * last_d[h, chain]
+        g = row(k_ref, h, k - 1 if chain else k) * r
+        g_ref[rows(h, k), :] = g
+        y_ref[rows(h, k), :] = d
+        last_d[h, chain] = d
+        last_g[h, chain] = g
+
+    chains = [(h, chain) for h in halves for chain in range(2)]
+    den, last_d, last_g = {}, {}, {}
+    for at in chains:
+        den[at] = base(*at, 0)
+        finish(*at, 0, 1.0 / den[at])
+    for step in range(1, HALF, 2):
+        for at in chains:
+            old = den[at]
+            k = link(*at, step)
+            r = 1.0 / (base(*at, step) * old - k * k)
+            if step + 1 < HALF:
+                k = link(*at, step + 1)
+                den[at] = base(*at, step + 1) - (k * k * old) * r
+            finish(*at, step, old * r)
+            if step + 1 < HALF:
+                finish(*at, step + 1, 1.0 / den[at])
     z = {}
     for h in halves:
-        d_up, d_dn = state[h, 0][2], state[h, 1][2]
-        g_up, g_dn = ends[h, 0], ends[h, 1]
+        d_up, d_dn = last_d[h, 0], last_d[h, 1]
+        g_up, g_dn = last_g[h, 0], last_g[h, 1]
         z[h, 0] = (d_up + g_up * d_dn) / (1.0 - g_up * g_dn)
         z[h, 1] = d_dn + g_dn * z[h, 0]
         y_ref[rows(h, HALF - 1), :] = z[h, 0]
@@ -225,16 +238,28 @@
     for h in range(COL // LANES):
         copies[h].wait()
         warm, mixed, icy = regimes(regime_ref, h)
-        above = jnp.zeros((8, LANES), f32)
+        above = [jnp.zeros((8, LANES), f32)] * 2
         for i in range(LEV // 8):
-            x = tuple(tile_ref[h, pl.ds(i * 64 + f, 8, stride=FLD), :] for f in range(5))
-            kept, source, excess, above = micro_free(x, warm, mixed, icy, above, top)
-            for f, value in enumerate(kept + (source, excess)):
+            x = [tile_ref[h, pl.ds(i * 64 + f, 8, stride=FLD), :] for f in range(7)]
+            rain_q, x[3], above[0] = rain_fall(x[3], above[0], top)
+            kept, source, excess = micro_free(x[:5], rain_q, warm, mixed, icy)
+            rain_q, rain, above[1] = rain_fall(kept[3], above[1], top)
+            shear = None
+            for f in (5, 6):
+                if i < LEV // 8 - 1:
+                    below = tile_ref[h, pl.ds(i * 64 + FLD + f, 8, stride=FLD), :]
+                else:
+                    below = pltpu.roll(x[f], 7, 0)
+                square = (x[f] - below) * (x[f] - below)
+                shear = square if shear is None else shear + square
+            shear = 1.5 * shear / (1.0 + shear)
+            values = kept[:3] + (rain, kept[4], source, excess, rain_q, shear)
+            for f, value in enumerate(values):
                 part_ref[h, f, i * 8 : i * 8 + 8, :] = value
     weights.wait()
     for n in range(4):
         down, across = (n % 2) * LANES, (n // 2) * LANES
-        for at, part in enumerate(split3(weight_own[n])):
+        for at, part in enumerate(split2(weight_own[n])):
             weight_part_ref[at, down : down + LANES, across : across + LANES] = part
     for copy in moments:
         copy.wait()
@@ -277,7 +302,7 @@
         [block_ref[p * DOWN * LEV : (p + 1) * DOWN * LEV, :] for p in range(CAP)], axis=1
     )
     total = None
-    for part in split3(slotted):
+    for part in split2(slotted):
         got = jnp.dot(part, hot_ref[...], preferred_element_type=f32)
         total = got if total is None else total + got
     mom_ref[0 : DOWN * LEV, :] = total
@@ -286,13 +311,12 @@
     for h in range(COL // LANES):
         lanes = slice(h * LANES, (h + 1) * LANES)
         warm, mixed, icy = regimes(regime_ref, h)
-        above = jnp.zeros((8, LANES), f32)
         base = h * PAD_ROWS
         for i in range(LEV // 8):
             m2 = mom_ref[LEV + i * 8 : LEV + i * 8 + 8, lanes]
-            first = tuple(part_ref[h, f, i * 8 : i * 8 + 8, :] for f in range(7))
+            first = tuple(part_ref[h, f, i * 8 : i * 8 + 8, :] for f in range(8))
             x = micro_bound(first[:5], first[5], first[6], m2, icy)
-            kept, source, excess, above = micro_free(x, warm, mixed, icy, above, top)
+            kept, source, excess = micro_free(x, first[7], warm, mixed, icy)
             x = micro_bound(kept, source, excess, m2, icy)
             for f, value in enumerate(x):
                 a_ref[pl.ds(base + i * 64 + f, 8, stride=FLD), :] = value
@@ -324,9 +348,13 @@
                         - src[pl.ds(first + FLD, 8, stride=FLD), :]
                     )
 
-                du, dv, dt = drop(5), drop(6), drop(0)
-                shear = du * du + dv * dv
-                mixing = 0.3 + 1.5 * shear / (1.0 + shear) * (0.5 - 0.5 * jnp.tanh(dt))
+                if turn == 0:
+                    shear = part_ref[h, 8, i * 8 : i * 8 + 8, :]
+                else:
+                    du, dv = drop(5), drop(6)
+                    shear = du * du + dv * dv
+                    shear = 1.5 * shear / (1.0 + shear)
+                mixing = 0.3 + shear * (0.5 - 0.5 * jnp.tanh(drop(0)))
                 kappa = mixing * e_ref[i * 8 : i * 8 + 8, lanes]
                 rolled = pltpu.roll(kappa, 1, 0)
                 k_ref[i * 8 : i * 8 + 8, lanes] = kappa
@@ -360,7 +388,7 @@
     for n in range(4):
         mine = jnp.where(cols_ref[n] == 0, flux[:, :LANES], flux[:, LANES:])
         used.append(jnp.concatenate([none, mine] if n % 2 else [mine, none], axis=1))
-    hi, mid, low = split3(jnp.concatenate(used, axis=0))
+    hi, low = split2(jnp.concatenate(used, axis=0))
 
     def weighted(parts, at):
         got = jnp.dot(
@@ -371,7 +399,7 @@
             total = total + got[i * 32 : i * 32 + 32, :]
         return total
 
-    products = weighted([hi], 2) + weighted([hi, mid], 1) + weighted([hi, mid, low], 0)
+    products = weighted([hi], 1) + weighted([hi, low], 0)
     odd = iota((PEERS, LANES), 0) % 2 == 1
     for n in range(2):
         for e in range(4):
@@ -404,7 +432,7 @@
         ],
         axis=1,
     )
-    parts = split3(fields)
+    parts = split2(fields)
     sent = 0
     for pair in range(CAP // 2):
         hot = hot_ref[pair * 2 * PEERS : (pair + 1) * 2 * PEERS, :]
@@ -447,7 +475,7 @@
         axis=0,
     )
     total = None
-    for part in split3(values):
+    for part in split2(values):
         got = jnp.dot(chosen, part, preferred_element_type=f32)
         total = got if total is None else total + got
     for e in range(4):
@@ -457,15 +485,18 @@
 
 
 def update_kernel(meta_ref, got_ref, tile_ref, out_ref, block_ref, new_ref, sem):
-    for t in range(ROWS_UP):
-        block_ref[8 + t * LANES : 8 + (t + 1) * LANES, :] = got_ref[
-            pl.ds(t, PEERS, stride=ROWS2), :
-        ].T
     count = meta_ref[4:5, :]
+    unpacked = 0
     top = iota((8, LANES), 0) == 0
     last = iota((8, LANES), 0) == 7
     copies = []
     for p in range(CAP):
+        needed = -(-(p + 1) * UP * LEV // LANES)
+        for t in range(unpacked, needed):
+            block_ref[8 + t * LANES : 8 + (t + 1) * LANES, :] = got_ref[
+                pl.ds(t, PEERS, stride=ROWS2), :
+            ].T
+        unpacked = needed
         live = jnp.broadcast_to(count, (8, LANES)) > p + 0.5
         for i in range(LEV // 8):
 
@@ -558,9 +589,9 @@
         [
             here((2, PLANE, LANES)),
             here((SLOTS, COL), bf16),
-            here((2, 7, LEV, LANES)),
+            here((2, PARTS, LEV, LANES)),
             here((CAP, PLANE, LANES)),
-            here((3, 2 * LANES, 2 * LANES), bf16),
+            here((2, 2 * LANES, 2 * LANES), bf16),
         ],
         [VMEM] * 5,
         [

time: 57.6 us -> 57 us (0.990)
  no operation moved by 1% of the time
where the time goes in v3:
time: 57 us; the launch traced here: 56.7 us
  blocking collectives  24.4 us (43%)
  starting transfers between devices  12.8 us (22%)
  waiting for transfers between devices  9.73 us (17%)
  Pallas kernels  8.42 us (15%)
  between operations  0.73 us (1%)
  other arithmetic  0.6 us (1%)
    all_to_all x1, blocking collectives, exchange(): lax.all_to_all(sent.reshape(PEERS, 1, rows * LANES), ('node', 'dev'), 0,...  24.4 us
    all_to_all x1, starting transfers between devices, exchange(): lax.all_to_all(sent.reshape(PEERS, 1, rows * LANES), ('node', 'dev'), 0,...  11.5 us
    all_to_all x1, waiting for transfers between devices, exchange(): lax.all_to_all(sent.reshape(PEERS, 1, rows * LANES), ('node', 'dev'), 0,...  9.73 us
    pallas_call x1, Pallas kernels, physics(): call(physics_kernel, [SMEM] * 2 + [VMEM] * 6, [far((PLANE, COL)), here((R...  3.25 us
    pallas_call x1, Pallas kernels, pack(): call(pack_kernel, [HBM] * 3, [here((ROWS1 * PEERS, LANES))], [VMEM], [plt...  1.95 us
    pallas_call x1, Pallas kernels, prepare(): call(prepare_kernel, [VMEM] * 2 + [HBM] * 3, [here((2, PLANE, LANES)), he...  1.68 us
    ppermute x1, starting transfers between devices, local(): other = lax.ppermute(send, 'dev', [(i, i ^ 1) for i in range(dev_count)])  1.34 us
    pallas_call x1, Pallas kernels, update(): call(update_kernel, [VMEM] * 3, [far((PLANE, SLOTS))], [ANY], [pltpu.VMEM...  1.33 us
  transfers between devices with their start and end apart: 2, of which 1 were waited for; matrix products, arithmetic and copies ran while one was open for 0% of the time, Pallas kernels for 5%

profile of v3, /device:TPU:1, one launch (start us, length us, event | category | flops | bytes accessed | tf_op | source)
XLA Modules:
  0.0 56.7 jit_solution(11775213970571999077)
XLA Ops:
  0.6 0.0 copy-start.1
  0.6 0.0 copy-start
  0.7 2.0 %pack.1 = f32[640,128]{1,0:T(8,128)} custom-call(s32[4]{0:T(128)} %rows_hbm.1, s32[1,256]{1,0:T(1,128)} %bitcast.17, f32[72,8,512]{2,1,0:T(8,128)} %mom_ref.1), custom_call_target="tpu_custom_call" | custom-call | tf_op jit(solution)/shard_map/pack/pallas_call | solution.py:569
  2.6 11.5 %all-to-all-start = ((f32[128,1,640]{2,1,0:T(1,128)}), f32[128,1,640]{2,1,0:T(1,128)S(1)}, u32[]{:S(2)}, u32[]{:S(2)}) async-start(f32[128,1,640]{2,1,0:T(1,128)} %bitcast.3), calls=%async_computation | async-start | bytes 655360 | tf_op jit(solution)/shard_map/all_to_all | solution.py:651
  14.1 0.0 copy-start.2
  14.1 0.0 copy-done.1
  14.1 0.0 copy-done
  14.1 1.7 %prepare.1 = (f32[2,576,128]{2,1,0:T(8,128)S(1)}, bf16[512,256]{1,0:T(8,128)(2,1)S(1)}, f32[2,9,72,128]{3,2,1,0:T(8,128)S(1)}, f32[4,576,128]{2,1,0:T(8,128)S(1)}, bf16[2,256,256]{2,1,0:T(8,128)(2,1)S(1)}) custom-call(s32[1,256]{1,0:T(1,128)S(1)} %bitcast.18, s32[1,256]{1,0:T(1,128)S(1)} %bitcast.15, f32[576,256]{1,0:T(8,128)} %bitcast.21, ...), custom_call_target="tpu_custom_call" | custom-call | tf_op jit(solution)/shard_map/prepare/pallas_call | solution.py:586
  15.8 9.7 %all-to-all-done = f32[128,1,640]{2,1,0:T(1,128)S(1)} async-done(((f32[128,1,640]{2,1,0:T(1,128)}), f32[128,1,640]{2,1,0:T(1,128)S(1)}, u32[]{:S(2)}, u32[]{:S(2)}) %all-to-all-start) | async-done | bytes 327712 | tf_op jit(solution)/shard_map/all_to_all | solution.py:651
  25.6 0.0 copy-done.2
  25.6 3.3 %physics.1 = (f32[576,256]{1,0:T(8,128)}, f32[2176,128]{1,0:T(8,128)S(1)}, f32[8,128]{1,0:T(8,128)S(1)}) custom-call(s32[1]{0:T(128)} %bitcast.device_ref, s32[4]{0:T(128)S(1)} %copy-done.2, s32[1,256]{1,0:T(1,128)S(1)} %bitcast.16, f32[640,128]{1,0:T(8,128)S(1)} %bitcast.13, f32[2,576,128]{2,1,0:T(8,128)S(1)} %get-tuple-element.13.tile_ref, ...), custom_call_target="tpu_custom_call" | custom-call | tf_op jit(solution)/shard_map/physics/pallas_call | solution.py:608
  28.8 24.4 %all_to_all.10 = f32[128,1,2176]{2,1,0:T(1,128)S(1)} all-to-all(f32[128,1,2176]{2,1,0:T(1,128)S(1)} %bitcast.14), channel_id=1, replica_groups=mesh['node'=4,'dev'=32] {'node','dev'}, dimensions={0} | all-to-all | bytes 2228224 | tf_op jit(solution)/shard_map/all_to_all | solution.py:651
  53.2 0.2 ocean.1
  53.5 1.3 %collective-permute-start = (f32[4,4,128]{2,1,0:T(4,128)S(1)}, f32[4,4,128]{2,1,0:T(4,128)S(1)}, u32[]{:S(2)}, u32[]{:S(2)}) collective-permute-start(f32[4,4,128]{2,1,0:T(4,128)S(1)} %get-tuple-element.22), channel_id=1, source_target_pairs={{0,1},{1,0},{2,3},{3,2},{4,5},{5,4},{6,7},{7,6},{8,9},{9,8},{10,11... | collective-permute-start | bytes 24584 | tf_op jit(solution)/shard_map/ppermute | solution.py:674
  54.8 1.3 %update.1 = f32[576,512]{1,0:T(8,128)} custom-call(f32[8,128]{1,0:T(8,128)S(1)} %get-tuple-element.18.meta_ref, f32[2176,128]{1,0:T(8,128)S(1)} %bitcast.12, f32[4,576,128]{2,1,0:T(8,128)S(1)} %get-tuple-element.20.tile_ref), custom_call_target="tpu_custom_call" | custom-call | tf_op jit(solution)/shard_map/update/pallas_call | solution.py:636
  56.1 0.0 collective-permute-done
  56.1 0.6 %add.7 = f32[4,4,128]{2,1,0:T(4,128)} add(f32[4,4,128]{2,1,0:T(4,128)S(1)} %get-tuple-element.21, f32[4,4,128]{2,1,0:T(4,128)S(1)} %collective-permute-done) | non-fusion elementwise | flops 2048 | bytes 24576 | tf_op jit(solution)/shard_map/add | solution.py:676
Async XLA Ops:
  0.6 13.5 %copy-start.1 = (s32[256,1]{0,1:T(1,128)S(1)}, s32[256,1]{0,1:T(1,128)}, u32[]{:S(2)}) copy-start(s32[256,1]{0,1:T(1,128)} %param.8) | copy-start | bytes 3076
  0.6 13.5 %copy-start = (s32[256]{0:T(256)S(1)}, s32[256]{0:T(256)}, u32[]{:S(2)}) copy-start(s32[256]{0:T(256)} %param.9) | copy-start | bytes 3076
  2.6 23.0 %all-to-all-start = ((f32[128,1,640]{2,1,0:T(1,128)}), f32[128,1,640]{2,1,0:T(1,128)S(1)}, u32[]{:S(2)}, u32[]{:S(2)}) async-start(f32[128,1,640]{2,1,0:T(1,128)} %bitcast.3), calls=%async_computation | async-start | bytes 655360 | tf_op jit(solution)/shard_map/all_to_all | solution.py:651
  14.1 11.5 %copy-start.2 = (s32[4]{0:T(128)S(1)}, s32[4]{0:T(128)}, u32[]{:S(2)}) copy-start(s32[4]{0:T(128)} %cols_ref.1) | copy-start | bytes 52
  53.5 2.7 %collective-permute-start = (f32[4,4,128]{2,1,0:T(4,128)S(1)}, f32[4,4,128]{2,1,0:T(4,128)S(1)}, u32[]{:S(2)}, u32[]{:S(2)}) collective-permute-start(f32[4,4,128]{2,1,0:T(4,128)S(1)} %get-tuple-element.22), channel_id=1, source_target_pairs={{0,1},{1,0},{2,3},{3,2},{4,5},{5,4},{6,7},{7,6},{8,9},{9,8},{10,11... | collective-permute-start | bytes 24584 | tf_op jit(solution)/shard_map/ppermute | solution.py:674

commit v4 on v3

--- a/solution.py
+++ b/solution.py
@@ -17,10 +17,12 @@
 ROWS1 = 5
 META = CAP * DOWN * LEV
 ROWS_UP = CAP * UP * LEV // LANES
-OCN_ROWS = 8
+OCN_ROWS = 4
+GROUP = 4
 ROWS2 = ROWS_UP + OCN_ROWS
 HALF = LEV // 2
-PAD_ROWS = LEV * FLD + FLD
+PITCH = 9
+PAD_ROWS = 664
 PARTS = 9
 f32 = jnp.float32
 bf16 = jnp.bfloat16
@@ -142,7 +144,7 @@
         return jnp.broadcast_to(one, (FLD, LANES))
 
     def rows(h, level):
-        first = h * PAD_ROWS + level * FLD
+        first = h * PAD_ROWS + level * PITCH
         return slice(first, first + FLD)
 
     def base(h, chain, step):
@@ -291,12 +293,18 @@
     for t in range(ROWS1):
         block_ref[t * LANES : (t + 1) * LANES, :] = got_ref[pl.ds(t, PEERS, stride=ROWS1), :].T
     device = device_ref[0]
-    core = device % 2
-    meta_ref[0:2, :] = jnp.where(
-        core == 1, block_ref[META + 2 : META + 4, :], block_ref[META : META + 2, :]
-    )
-    meta_ref[2:3, :] = jnp.full((1, PEERS), (device * 4).astype(f32))
-    meta_ref[3:4, :] = jnp.full((1, PEERS), ((device + 1 - 2 * core) * 4).astype(f32))
+    mine = device % GROUP
+    picked = block_ref[META : META + 1, :]
+    for n in range(1, 4):
+        picked = jnp.where(mine == n, block_ref[META + n : META + n + 1, :], picked)
+    meta_ref[0:1, :] = picked
+    group = device - mine
+    member = iota((16, PEERS), 0) // 4
+    first_row = jnp.zeros((16, PEERS), f32)
+    for flip in range(GROUP):
+        partner = group + mine + flip - 2 * (mine & flip)
+        first_row = jnp.where(member == flip, (partner * 4).astype(f32), first_row)
+    meta_ref[8:24, :] = first_row + (iota((16, PEERS), 0) % 4).astype(f32)
     meta_ref[4:8, :] = block_ref[META + 4 : META + 8, :]
     slotted = jnp.concatenate(
         [block_ref[p * DOWN * LEV : (p + 1) * DOWN * LEV, :] for p in range(CAP)], axis=1
@@ -319,13 +327,13 @@
             kept, source, excess = micro_free(x, first[7], warm, mixed, icy)
             x = micro_bound(kept, source, excess, m2, icy)
             for f, value in enumerate(x):
-                a_ref[pl.ds(base + i * 64 + f, 8, stride=FLD), :] = value
+                a_ref[pl.ds(base + i * 8 * PITCH + f, 8, stride=PITCH), :] = value
             for f in range(5, FLD):
-                a_ref[pl.ds(base + i * 64 + f, 8, stride=FLD), :] = tile_ref[
+                a_ref[pl.ds(base + i * 8 * PITCH + f, 8, stride=PITCH), :] = tile_ref[
                     h, pl.ds(i * 64 + f, 8, stride=FLD), :
                 ]
         for ref in (a_ref, y_ref):
-            ref[base + LEV * FLD : base + PAD_ROWS, :] = jnp.zeros((FLD, LANES), f32)
+            ref[base + LEV * PITCH : base + LEV * PITCH + FLD, :] = jnp.zeros((FLD, LANES), f32)
     last = iota((8, COL), 0) == 7
     for i in range(LEV // 8):
         m0 = mom_ref[i * 8 : i * 8 + 8, :]
@@ -342,10 +350,10 @@
             for i in range(LEV // 8):
 
                 def drop(f):
-                    first = h * PAD_ROWS + i * 64 + f
+                    first = h * PAD_ROWS + i * 8 * PITCH + f
                     return (
-                        src[pl.ds(first, 8, stride=FLD), :]
-                        - src[pl.ds(first + FLD, 8, stride=FLD), :]
+                        src[pl.ds(first, 8, stride=PITCH), :]
+                        - src[pl.ds(first + PITCH, 8, stride=PITCH), :]
                     )
 
                 if turn == 0:
@@ -367,7 +375,8 @@
     bottom = []
     for h in range(COL // LANES):
         level = slice((LEV - 1) * FLD, LEV * FLD)
-        at = slice(h * PAD_ROWS + (LEV - 1) * FLD, h * PAD_ROWS + LEV * FLD)
+        first = h * PAD_ROWS + (LEV - 1) * PITCH
+        at = slice(first, first + FLD)
         old = tile_ref[h, level, :]
         bottom.append(old + (jnp.where(kept, a_ref[at, :], y_ref[at, :]) - old))
     b = jnp.concatenate(bottom, axis=1)
@@ -400,20 +409,20 @@
         return total
 
     products = weighted([hi], 1) + weighted([hi, low], 0)
-    odd = iota((PEERS, LANES), 0) % 2 == 1
-    for n in range(2):
-        for e in range(4):
-            even_row = products[n * 8 + e : n * 8 + e + 1, 0:LANES]
-            odd_row = products[n * 8 + 16 + e : n * 8 + 17 + e, LANES:]
-            out_ref[pl.ds(ROWS_UP + 4 * n + e, PEERS, stride=ROWS2), :] = jnp.where(
-                odd, odd_row, even_row
-            )
+    which = iota((PEERS, LANES), 0) % GROUP
+    for e in range(4):
+        value = jnp.broadcast_to(products[e : e + 1, 0:LANES], (PEERS, LANES))
+        for n in range(1, 4):
+            across = (n // 2) * LANES
+            other = products[n * 8 + e : n * 8 + e + 1, across : across + LANES]
+            value = jnp.where(which == n, other, value)
+        out_ref[pl.ds(ROWS_UP + e, PEERS, stride=ROWS2), :] = value
 
     copies = []
     for h in range(COL // LANES):
         for k in range(LEV):
             rows = slice(k * FLD, (k + 1) * FLD)
-            at = slice(h * PAD_ROWS + k * FLD, h * PAD_ROWS + (k + 1) * FLD)
+            at = slice(h * PAD_ROWS + k * PITCH, h * PAD_ROWS + k * PITCH + FLD)
             mixed_state = jnp.where(kept, a_ref[at, :], y_ref[at, :])
             tend_ref[h, rows, :] = mixed_state - tile_ref[h, rows, :]
         copies.append(
@@ -426,7 +435,7 @@
     fields = jnp.concatenate(
         [
             jnp.concatenate(
-                [y_ref[pl.ds(h * PAD_ROWS + f, LEV, stride=FLD), :] for f in (0, 1, 5, 6)], axis=0
+                [y_ref[pl.ds(h * PAD_ROWS + f, LEV, stride=PITCH), :] for f in (0, 1, 5, 6)], axis=0
             )
             for h in range(COL // LANES)
         ],
@@ -455,33 +464,20 @@
         copy.wait()
 
 
-def ocean_kernel(meta_ref, got_ref, keep_ref, send_ref):
-    row = iota((8, PEERS), 0).astype(f32)
-    wanted = jnp.where(row < 3.5, meta_ref[2:3, :] + row, meta_ref[3:4, :] + (row - 4.0))
-    chosen = jnp.concatenate(
-        [(meta_ref[n : n + 1, :] == wanted).astype(bf16) for n in range(2)], axis=1
-    )
+def ocean_kernel(meta_ref, got_ref, *sum_refs):
+    chosen = (meta_ref[0:1, :] == meta_ref[8:24, :]).astype(bf16)
     values = jnp.concatenate(
-        [
-            jnp.concatenate(
-                [
-                    got_ref[pl.ds(ROWS_UP + 4 * n + e, PEERS, stride=ROWS2), :]
-                    for e in range(4)
-                ],
-                axis=1,
-            )
-            for n in range(2)
-        ],
-        axis=0,
+        [got_ref[pl.ds(ROWS_UP + e, PEERS, stride=ROWS2), :] for e in range(4)], axis=1
     )
     total = None
     for part in split2(values):
         got = jnp.dot(chosen, part, preferred_element_type=f32)
         total = got if total is None else total + got
     for e in range(4):
-        part = total[:, e * LANES : (e + 1) * LANES]
-        keep_ref[:, e, :] = part[0:4, :]
-        send_ref[:, e, :] = part[4:8, :]
+        for flip in range(GROUP):
+            sum_refs[flip][:, e, :] = total[
+                flip * 4 : flip * 4 + 4, e * LANES : (e + 1) * LANES
+            ]
 
 
 def update_kernel(meta_ref, got_ref, tile_ref, out_ref, block_ref, new_ref, sem):
@@ -517,7 +513,7 @@
             for j in range(FLD):
                 at = pl.ds(i * 64 + j, 8, stride=FLD)
                 m = tile_ref[p, at, :]
-                new = m + 0.5 * (jnp.tanh(production[j]) - (0.3 + 0.1 * j) * m)
+                new = (0.85 - 0.05 * j) * m + 0.5 * jnp.tanh(production[j])
                 new_ref[p, at, :] = jnp.where(live, new, m)
         copies.append(
             pltpu.make_async_copy(
@@ -608,7 +604,7 @@
     return call(
         physics_kernel,
         [SMEM] * 2 + [VMEM] * 6,
-        [far((PLANE, COL)), here((ROWS2 * PEERS, LANES)), here((8, PEERS))],
+        [far((PLANE, COL)), here((ROWS2 * PEERS, LANES)), here((24, PEERS))],
         [ANY, VMEM, VMEM],
         [
             pltpu.VMEM((2, PLANE, LANES), f32),
@@ -628,7 +624,7 @@
 
 def ocean(meta, back):
     return call(
-        ocean_kernel, [VMEM, VMEM], [here((4, 4, LANES))] * 2, [VMEM] * 2, [], "ocean"
+        ocean_kernel, [VMEM, VMEM], [here((4, 4, LANES))] * GROUP, [VMEM] * GROUP, [], "ocean"
     )(hold(meta), hold(back))
 
 
@@ -670,10 +666,14 @@
     got = exchange(sent, ROWS1)
     tend, sent, meta = physics(device, remap_cols, regime_row, got, tiles, hot, parts, weights)
     back = exchange(sent, ROWS2)
-    keep, send = ocean(meta, back)
-    other = lax.ppermute(send, "dev", [(i, i ^ 1) for i in range(dev_count)])
+    sums = ocean(meta, back)
+    others = [
+        lax.ppermute(sums[flip], "dev", [(i, i ^ flip) for i in range(dev_count)])
+        for flip in (2, 3, 1)
+    ]
     new_mom = update(meta, back, mom_tiles)
-    return tend.reshape(LEV, FLD, COL), new_mom.reshape(LEV, FLD, SLOTS), keep + other
+    flux = sums[0] + others[2] + others[0] + others[1]
+    return tend.reshape(LEV, FLD, COL), new_mom.reshape(LEV, FLD, SLOTS), flux
 
 
 def solution(mesh):

time: 57 us -> 56.1 us (0.984)
  blocking collectives: 24.4 us -> 21.6 us
  starting transfers between devices: 12.8 us -> 14.5 us
    all_to_all x1, blocking collectives: 24.4 us -> 21.6 us  [exchange(): lax.all_to_all(sent.reshape(PEERS, 1, rows * LANES), ('node', 'dev'), 0,...]
    ppermute x1 -> x3, starting transfers between devices: 1.34 us -> 3.02 us  [local(): lax.ppermute(sums[flip], 'dev', [(i, i ^ flip) for i in range(dev_count)])]
  transfers between devices with their start and end apart: 2 -> 4, of which waited for: 1 -> 2; matrix products, arithmetic and copies ran while one was open for 0% -> 0% of each run, Pallas kernels for 5% -> 5%
where the time goes in v4:
time: 56.1 us; the launch traced here: 55.9 us
  blocking collectives  21.6 us (39%)
  starting transfers between devices  14.5 us (26%)
  waiting for transfers between devices  10 us (18%)
  Pallas kernels  8.34 us (15%)
  between operations  0.74 us (1%)
  other arithmetic  0.6 us (1%)
    all_to_all x1, blocking collectives, exchange(): lax.all_to_all(sent.reshape(PEERS, 1, rows * LANES), ('node', 'dev'), 0,...  21.6 us
    all_to_all x1, starting transfers between devices, exchange(): lax.all_to_all(sent.reshape(PEERS, 1, rows * LANES), ('node', 'dev'), 0,...  11.5 us
    all_to_all x1, waiting for transfers between devices, exchange(): lax.all_to_all(sent.reshape(PEERS, 1, rows * LANES), ('node', 'dev'), 0,...  9.73 us
    pallas_call x1, Pallas kernels, physics(): call(physics_kernel, [SMEM] * 2 + [VMEM] * 6, [far((PLANE, COL)), here((R...  3.22 us
    ppermute x3, starting transfers between devices, local(): lax.ppermute(sums[flip], 'dev', [(i, i ^ flip) for i in range(dev_count)])  3.02 us
    pallas_call x1, Pallas kernels, pack(): call(pack_kernel, [HBM] * 3, [here((ROWS1 * PEERS, LANES))], [VMEM], [plt...  1.95 us
    pallas_call x1, Pallas kernels, prepare(): call(prepare_kernel, [VMEM] * 2 + [HBM] * 3, [here((2, PLANE, LANES)), he...  1.68 us
    pallas_call x1, Pallas kernels, update(): call(update_kernel, [VMEM] * 3, [far((PLANE, SLOTS))], [ANY], [pltpu.VMEM...  1.31 us
  transfers between devices with their start and end apart: 4, of which 2 were waited for; matrix products, arithmetic and copies ran while one was open for 0% of the time, Pallas kernels for 5%

profile of v4, /device:TPU:1, one launch (start us, length us, event | category | flops | bytes accessed | tf_op | source)
XLA Modules:
  0.0 55.9 jit_solution(17439603677173382811)
XLA Ops:
  0.6 0.0 copy-start.1
  0.6 0.0 copy-start
  0.7 2.0 %pack.1 = f32[640,128]{1,0:T(8,128)} custom-call(s32[4]{0:T(128)} %rows_hbm.1, s32[1,256]{1,0:T(1,128)} %bitcast.23, f32[72,8,512]{2,1,0:T(8,128)} %mom_ref.1), custom_call_target="tpu_custom_call" | custom-call | tf_op jit(solution)/shard_map/pack/pallas_call | solution.py:565
  2.6 11.5 %all-to-all-start = ((f32[128,1,640]{2,1,0:T(1,128)}), f32[128,1,640]{2,1,0:T(1,128)S(1)}, u32[]{:S(2)}, u32[]{:S(2)}) async-start(f32[128,1,640]{2,1,0:T(1,128)} %bitcast.3), calls=%async_computation | async-start | bytes 655360 | tf_op jit(solution)/shard_map/all_to_all | solution.py:647
  14.1 0.0 copy-start.2
  14.1 0.0 copy-done.1
  14.1 0.0 copy-done
  14.1 1.7 %prepare.1 = (f32[2,576,128]{2,1,0:T(8,128)S(1)}, bf16[512,256]{1,0:T(8,128)(2,1)S(1)}, f32[2,9,72,128]{3,2,1,0:T(8,128)S(1)}, f32[4,576,128]{2,1,0:T(8,128)S(1)}, bf16[2,256,256]{2,1,0:T(8,128)(2,1)S(1)}) custom-call(s32[1,256]{1,0:T(1,128)S(1)} %bitcast.24, s32[1,256]{1,0:T(1,128)S(1)} %bitcast.21, f32[576,256]{1,0:T(8,128)} %bitcast.27, ...), custom_call_target="tpu_custom_call" | custom-call | tf_op jit(solution)/shard_map/prepare/pallas_call | solution.py:582
  15.8 9.7 %all-to-all-done = f32[128,1,640]{2,1,0:T(1,128)S(1)} async-done(((f32[128,1,640]{2,1,0:T(1,128)}), f32[128,1,640]{2,1,0:T(1,128)S(1)}, u32[]{:S(2)}, u32[]{:S(2)}) %all-to-all-start) | async-done | bytes 327712 | tf_op jit(solution)/shard_map/all_to_all | solution.py:647
  25.6 0.0 copy-done.2
  25.6 3.2 %physics.1 = (f32[576,256]{1,0:T(8,128)}, f32[1664,128]{1,0:T(8,128)S(1)}, f32[24,128]{1,0:T(8,128)S(1)}) custom-call(s32[1]{0:T(128)} %bitcast.device_ref, s32[4]{0:T(128)S(1)} %copy-done.2, s32[1,256]{1,0:T(1,128)S(1)} %bitcast.22, f32[640,128]{1,0:T(8,128)S(1)} %bitcast.18, f32[2,576,128]{2,1,0:T(8,128)S(1)} %get-tuple-element.15.tile_ref, ...), custom_call_target="tpu_custom_call" | custom-call | tf_op jit(solution)/shard_map/physics/pallas_call | solution.py:604
  28.8 21.6 %all_to_all.10 = f32[128,1,1664]{2,1,0:T(1,128)S(1)} all-to-all(f32[128,1,1664]{2,1,0:T(1,128)S(1)} %bitcast.19), channel_id=1, replica_groups=mesh['node'=4,'dev'=32] {'node','dev'}, dimensions={0} | all-to-all | bytes 1703936 | tf_op jit(solution)/shard_map/all_to_all | solution.py:647
  50.4 0.2 ocean.1
  50.6 1.3 %collective-permute-start = (f32[4,4,128]{2,1,0:T(4,128)S(1)}, f32[4,4,128]{2,1,0:T(4,128)S(1)}, u32[]{:S(2)}, u32[]{:S(2)}) collective-permute-start(f32[4,4,128]{2,1,0:T(4,128)S(1)} %get-tuple-element.24), channel_id=1, source_target_pairs={{0,1},{1,0},{2,3},{3,2},{4,5},{5,4},{6,7},{7,6},{8,9},{9,8},{10,11... | collective-permute-start | bytes 24584 | tf_op jit(solution)/shard_map/ppermute | solution.py:671
  51.9 0.0 collective-permute-start.1
  51.9 1.7 %collective-permute-start.2 = (f32[4,4,128]{2,1,0:T(4,128)S(1)}, f32[4,4,128]{2,1,0:T(4,128)S(1)}, u32[]{:S(2)}, u32[]{:S(2)}) collective-permute-start(f32[4,4,128]{2,1,0:T(4,128)S(1)} %get-tuple-element.26), channel_id=1, source_target_pairs={{0,3},{1,2},{2,1},{3,0},{4,7},{5,6},{6,5},{7,4},{8,11},{9,10},{10,... | collective-permute-start | bytes 24584 | tf_op jit(solution)/shard_map/ppermute | solution.py:671
  53.6 1.3 %update.1 = f32[576,512]{1,0:T(8,128)} custom-call(f32[24,128]{1,0:T(8,128)S(1)} %get-tuple-element.20.meta_ref, f32[1664,128]{1,0:T(8,128)S(1)} %bitcast.17, f32[4,576,128]{2,1,0:T(8,128)S(1)} %get-tuple-element.22.tile_ref), custom_call_target="tpu_custom_call" | custom-call | tf_op jit(solution)/shard_map/update/pallas_call | solution.py:632
  55.0 0.0 collective-permute-done
  55.0 0.0 collective-permute-done.1
  55.0 0.3 collective-permute-done.2
  55.3 0.6 %add_add_fusion = f32[2,8,128]{2,1,0:T(8,128)} fusion(f32[2,8,128]{2,1,0:T(8,128)S(1)} %bitcast.30, f32[2,8,128]{2,1,0:T(8,128)S(1)} %bitcast.29, f32[2,8,128]{2,1,0:T(8,128)S(1)} %bitcast.20, f32[2,8,128]{2,1,0:T(8,128)S(1)} %bitcast.28), kind=kLoop, calls=%fused_computation | loop fusion | flops 6144 | bytes 40960 | tf_op jit(solution)/shard_map/add | solution.py:675
Async XLA Ops:
  0.6 13.5 %copy-start.1 = (s32[256,1]{0,1:T(1,128)S(1)}, s32[256,1]{0,1:T(1,128)}, u32[]{:S(2)}) copy-start(s32[256,1]{0,1:T(1,128)} %param.8) | copy-start | bytes 3076
  0.6 13.5 %copy-start = (s32[256]{0:T(256)S(1)}, s32[256]{0:T(256)}, u32[]{:S(2)}) copy-start(s32[256]{0:T(256)} %param.9) | copy-start | bytes 3076
  2.6 23.0 %all-to-all-start = ((f32[128,1,640]{2,1,0:T(1,128)}), f32[128,1,640]{2,1,0:T(1,128)S(1)}, u32[]{:S(2)}, u32[]{:S(2)}) async-start(f32[128,1,640]{2,1,0:T(1,128)} %bitcast.3), calls=%async_computation | async-start | bytes 655360 | tf_op jit(solution)/shard_map/all_to_all | solution.py:647
  14.1 11.5 %copy-start.2 = (s32[4]{0:T(128)S(1)}, s32[4]{0:T(128)}, u32[]{:S(2)}) copy-start(s32[4]{0:T(128)} %cols_ref.1) | copy-start | bytes 52
  50.6 4.3 %collective-permute-start = (f32[4,4,128]{2,1,0:T(4,128)S(1)}, f32[4,4,128]{2,1,0:T(4,128)S(1)}, u32[]{:S(2)}, u32[]{:S(2)}) collective-permute-start(f32[4,4,128]{2,1,0:T(4,128)S(1)} %get-tuple-element.24), channel_id=1, source_target_pairs={{0,1},{1,0},{2,3},{3,2},{4,5},{5,4},{6,7},{7,6},{8,9},{9,8},{10,11... | collective-permute-start | bytes 24584 | tf_op jit(solution)/shard_map/ppermute | solution.py:671
  51.9 3.1 %collective-permute-start.1 = (f32[4,4,128]{2,1,0:T(4,128)S(1)}, f32[4,4,128]{2,1,0:T(4,128)S(1)}, u32[]{:S(2)}, u32[]{:S(2)}) collective-permute-start(f32[4,4,128]{2,1,0:T(4,128)S(1)} %get-tuple-element.25), channel_id=1, source_target_pairs={{0,2},{1,3},{2,0},{3,1},{4,6},{5,7},{6,4},{7,5},{8,10},{9,11},{10,... | collective-permute-start | bytes 24584 | tf_op jit(solution)/shard_map/ppermute | solution.py:671
  51.9 3.3 %collective-permute-start.2 = (f32[4,4,128]{2,1,0:T(4,128)S(1)}, f32[4,4,128]{2,1,0:T(4,128)S(1)}, u32[]{:S(2)}, u32[]{:S(2)}) collective-permute-start(f32[4,4,128]{2,1,0:T(4,128)S(1)} %get-tuple-element.26), channel_id=1, source_target_pairs={{0,3},{1,2},{2,1},{3,0},{4,7},{5,6},{6,5},{7,4},{8,11},{9,10},{10,... | collective-permute-start | bytes 24584 | tf_op jit(solution)/shard_map/ppermute | solution.py:671

commit v5 on v4

--- a/solution.py
+++ b/solution.py
@@ -4,6 +4,7 @@
 from jax.experimental import pallas as pl
 from jax.experimental.pallas import tpu as pltpu
 from jax.sharding import PartitionSpec as P
+
 
 LEV = 72
 FLD = 8
@@ -549,14 +550,13 @@
     return pltpu.with_memory_space_constraint(x, pltpu.HBM)
 
 
-def call(kernel, ins, outs, out_specs, scratch, name):
+def call(kernel, ins, outs, out_specs, scratch):
     return pl.pallas_call(
         kernel,
         in_specs=ins,
         out_specs=out_specs,
         out_shape=outs,
         scratch_shapes=scratch,
-        name=name,
         compiler_params=pltpu.CompilerParams(vmem_limit_bytes=VMEM_LIMIT),
     )
 
@@ -574,7 +574,6 @@
             pltpu.SemaphoreType.DMA((CAP, DOWN)),
             pltpu.SemaphoreType.DMA((2,)),
         ],
-        "pack",
     )(outside(rows), outside(owner_row), outside(mom))[0]
 
 
@@ -596,7 +595,6 @@
             pltpu.SemaphoreType.DMA((CAP,)),
             pltpu.SemaphoreType.DMA,
         ],
-        "prepare",
     )(owner_row, regime_row, outside(state), outside(mom), outside(weights))
 
 
@@ -618,13 +616,12 @@
             pltpu.VMEM((LEV, COL), f32),
             pltpu.SemaphoreType.DMA((2,)),
         ],
-        "physics",
     )(device, cols, regime_row, *(hold(x) for x in (got, tiles, hot, parts, weights)))
 
 
 def ocean(meta, back):
     return call(
-        ocean_kernel, [VMEM, VMEM], [here((4, 4, LANES))] * GROUP, [VMEM] * GROUP, [], "ocean"
+        ocean_kernel, [VMEM, VMEM], [here((4, 4, LANES))] * GROUP, [VMEM] * GROUP, []
     )(hold(meta), hold(back))
 
 
@@ -639,7 +636,6 @@
             pltpu.VMEM((CAP, PLANE, LANES), f32),
             pltpu.SemaphoreType.DMA((CAP,)),
         ],
-        "update",
     )(hold(meta), hold(back), hold(tiles))[0]
 
 
@@ -667,10 +663,9 @@
     tend, sent, meta = physics(device, remap_cols, regime_row, got, tiles, hot, parts, weights)
     back = exchange(sent, ROWS2)
     sums = ocean(meta, back)
-    others = [
-        lax.ppermute(sums[flip], "dev", [(i, i ^ flip) for i in range(dev_count)])
-        for flip in (2, 3, 1)
-    ]
+    others = []
+    for flip in (2, 3, 1):
+        others.append(lax.ppermute(sums[flip], "dev", [(i, i ^ flip) for i in range(dev_count)]))
     new_mom = update(meta, back, mom_tiles)
     flux = sums[0] + others[2] + others[0] + others[1]
     return tend.reshape(LEV, FLD, COL), new_mom.reshape(LEV, FLD, SLOTS), flux

time: 56.1 us -> 56.1 us (level)
  no operation moved by 1% of the time
where the time goes in v5:
time: 56.1 us; the launch traced here: 55.9 us
  blocking collectives  21.6 us (39%)
  starting transfers between devices  14.5 us (26%)
  waiting for transfers between devices  10 us (18%)
  Pallas kernels  8.34 us (15%)
  between operations  0.74 us (1%)
  other arithmetic  0.6 us (1%)
    all_to_all x1, blocking collectives, exchange(): lax.all_to_all(sent.reshape(PEERS, 1, rows * LANES), ('node', 'dev'), 0,...  21.6 us
    all_to_all x1, starting transfers between devices, exchange(): lax.all_to_all(sent.reshape(PEERS, 1, rows * LANES), ('node', 'dev'), 0,...  11.5 us
    all_to_all x1, waiting for transfers between devices, exchange(): lax.all_to_all(sent.reshape(PEERS, 1, rows * LANES), ('node', 'dev'), 0,...  9.73 us
    pallas_call x1, Pallas kernels, physics(): call(physics_kernel, [SMEM] * 2 + [VMEM] * 6, [far((PLANE, COL)), here((R...  3.22 us
    ppermute x3, starting transfers between devices, local(): lax.ppermute(sums[flip], 'dev', [(i, i ^ flip) for i in range(dev_count)])  3.02 us
    pallas_call x1, Pallas kernels, pack(): call(pack_kernel, [HBM] * 3, [here((ROWS1 * PEERS, LANES))], [VMEM], [plt...  1.95 us
    pallas_call x1, Pallas kernels, prepare(): call(prepare_kernel, [VMEM] * 2 + [HBM] * 3, [here((2, PLANE, LANES)), he...  1.68 us
    pallas_call x1, Pallas kernels, update(): call(update_kernel, [VMEM] * 3, [far((PLANE, SLOTS))], [ANY], [pltpu.VMEM...  1.31 us
  transfers between devices with their start and end apart: 4, of which 2 were waited for; matrix products, arithmetic and copies ran while one was open for 0% of the time, Pallas kernels for 5%

profile of v5, /device:TPU:1, one launch (start us, length us, event | category | flops | bytes accessed | tf_op | source)
XLA Modules:
  0.0 55.9 jit_solution(17439603677173382811)
XLA Ops:
  0.6 0.0 copy-start.1
  0.6 0.0 copy-start
  0.7 2.0 %shard_map.94 = f32[640,128]{1,0:T(8,128)} custom-call(s32[4]{0:T(128)} %rows_hbm.1, s32[1,256]{1,0:T(1,128)} %bitcast.23, f32[72,8,512]{2,1,0:T(8,128)} %mom_ref.1), custom_call_target="tpu_custom_call" | custom-call | tf_op jit(solution)/shard_map/pallas_call | solution.py:565
  2.6 11.5 %all-to-all-start = ((f32[128,1,640]{2,1,0:T(1,128)}), f32[128,1,640]{2,1,0:T(1,128)S(1)}, u32[]{:S(2)}, u32[]{:S(2)}) async-start(f32[128,1,640]{2,1,0:T(1,128)} %bitcast.3), calls=%async_computation | async-start | bytes 655360 | tf_op jit(solution)/shard_map/all_to_all | solution.py:643
  14.1 0.0 copy-start.2
  14.1 0.0 copy-done.1
  14.1 0.0 copy-done
  14.1 1.7 %shard_map.95 = (f32[2,576,128]{2,1,0:T(8,128)S(1)}, bf16[512,256]{1,0:T(8,128)(2,1)S(1)}, f32[2,9,72,128]{3,2,1,0:T(8,128)S(1)}, f32[4,576,128]{2,1,0:T(8,128)S(1)}, bf16[2,256,256]{2,1,0:T(8,128)(2,1)S(1)}) custom-call(s32[1,256]{1,0:T(1,128)S(1)} %bitcast.24, s32[1,256]{1,0:T(1,128)S(1)} %bitcast.21, f32[576,256]{1,0:T(8,128)} %bitcast.27, ...), custom_call_target="tpu_custom_call" | custom-call | tf_op jit(solution)/shard_map/pallas_call | solution.py:581
  15.8 9.7 %all-to-all-done = f32[128,1,640]{2,1,0:T(1,128)S(1)} async-done(((f32[128,1,640]{2,1,0:T(1,128)}), f32[128,1,640]{2,1,0:T(1,128)S(1)}, u32[]{:S(2)}, u32[]{:S(2)}) %all-to-all-start) | async-done | bytes 327712 | tf_op jit(solution)/shard_map/all_to_all | solution.py:643
  25.6 0.0 copy-done.2
  25.6 3.2 %shard_map.96 = (f32[576,256]{1,0:T(8,128)}, f32[1664,128]{1,0:T(8,128)S(1)}, f32[24,128]{1,0:T(8,128)S(1)}) custom-call(s32[1]{0:T(128)} %bitcast.device_ref, s32[4]{0:T(128)S(1)} %copy-done.2, s32[1,256]{1,0:T(1,128)S(1)} %bitcast.22, f32[640,128]{1,0:T(8,128)S(1)} %bitcast.18, f32[2,576,128]{2,1,0:T(8,128)S(1)} %get-tuple-element.15.tile_ref, ...), custom_call_target="tpu_custom_call" | custom-call | tf_op jit(solution)/shard_map/pallas_call | solution.py:602
  28.8 21.6 %all_to_all.10 = f32[128,1,1664]{2,1,0:T(1,128)S(1)} all-to-all(f32[128,1,1664]{2,1,0:T(1,128)S(1)} %bitcast.19), channel_id=1, replica_groups=mesh['node'=4,'dev'=32] {'node','dev'}, dimensions={0} | all-to-all | bytes 1703936 | tf_op jit(solution)/shard_map/all_to_all | solution.py:643
  50.4 0.2 shard_map.98
  50.6 1.3 %collective-permute-start = (f32[4,4,128]{2,1,0:T(4,128)S(1)}, f32[4,4,128]{2,1,0:T(4,128)S(1)}, u32[]{:S(2)}, u32[]{:S(2)}) collective-permute-start(f32[4,4,128]{2,1,0:T(4,128)S(1)} %get-tuple-element.24), channel_id=1, source_target_pairs={{0,1},{1,0},{2,3},{3,2},{4,5},{5,4},{6,7},{7,6},{8,9},{9,8},{10,11... | collective-permute-start | bytes 24584 | tf_op jit(solution)/shard_map/ppermute | solution.py:668
  51.9 0.0 collective-permute-start.1
  51.9 1.7 %collective-permute-start.2 = (f32[4,4,128]{2,1,0:T(4,128)S(1)}, f32[4,4,128]{2,1,0:T(4,128)S(1)}, u32[]{:S(2)}, u32[]{:S(2)}) collective-permute-start(f32[4,4,128]{2,1,0:T(4,128)S(1)} %get-tuple-element.26), channel_id=1, source_target_pairs={{0,3},{1,2},{2,1},{3,0},{4,7},{5,6},{6,5},{7,4},{8,11},{9,10},{10,... | collective-permute-start | bytes 24584 | tf_op jit(solution)/shard_map/ppermute | solution.py:668
  53.6 1.3 %shard_map.97 = f32[576,512]{1,0:T(8,128)} custom-call(f32[24,128]{1,0:T(8,128)S(1)} %get-tuple-element.20.meta_ref, f32[1664,128]{1,0:T(8,128)S(1)} %bitcast.17, f32[4,576,128]{2,1,0:T(8,128)S(1)} %get-tuple-element.22.tile_ref), custom_call_target="tpu_custom_call" | custom-call | tf_op jit(solution)/shard_map/pallas_call | solution.py:629
  55.0 0.0 collective-permute-done
  55.0 0.0 collective-permute-done.1
  55.0 0.3 collective-permute-done.2
  55.3 0.6 %add_add_fusion = f32[2,8,128]{2,1,0:T(8,128)} fusion(f32[2,8,128]{2,1,0:T(8,128)S(1)} %bitcast.30, f32[2,8,128]{2,1,0:T(8,128)S(1)} %bitcast.29, f32[2,8,128]{2,1,0:T(8,128)S(1)} %bitcast.20, f32[2,8,128]{2,1,0:T(8,128)S(1)} %bitcast.28), kind=kLoop, calls=%fused_computation | loop fusion | flops 6144 | bytes 40960 | tf_op jit(solution)/shard_map/add | solution.py:670
Async XLA Ops:
  0.6 13.5 %copy-start.1 = (s32[256,1]{0,1:T(1,128)S(1)}, s32[256,1]{0,1:T(1,128)}, u32[]{:S(2)}) copy-start(s32[256,1]{0,1:T(1,128)} %param.8) | copy-start | bytes 3076
  0.6 13.5 %copy-start = (s32[256]{0:T(256)S(1)}, s32[256]{0:T(256)}, u32[]{:S(2)}) copy-start(s32[256]{0:T(256)} %param.9) | copy-start | bytes 3076
  2.6 23.0 %all-to-all-start = ((f32[128,1,640]{2,1,0:T(1,128)}), f32[128,1,640]{2,1,0:T(1,128)S(1)}, u32[]{:S(2)}, u32[]{:S(2)}) async-start(f32[128,1,640]{2,1,0:T(1,128)} %bitcast.3), calls=%async_computation | async-start | bytes 655360 | tf_op jit(solution)/shard_map/all_to_all | solution.py:643
  14.1 11.5 %copy-start.2 = (s32[4]{0:T(128)S(1)}, s32[4]{0:T(128)}, u32[]{:S(2)}) copy-start(s32[4]{0:T(128)} %cols_ref.1) | copy-start | bytes 52
  50.6 4.3 %collective-permute-start = (f32[4,4,128]{2,1,0:T(4,128)S(1)}, f32[4,4,128]{2,1,0:T(4,128)S(1)}, u32[]{:S(2)}, u32[]{:S(2)}) collective-permute-start(f32[4,4,128]{2,1,0:T(4,128)S(1)} %get-tuple-element.24), channel_id=1, source_target_pairs={{0,1},{1,0},{2,3},{3,2},{4,5},{5,4},{6,7},{7,6},{8,9},{9,8},{10,11... | collective-permute-start | bytes 24584 | tf_op jit(solution)/shard_map/ppermute | solution.py:668
  51.9 3.1 %collective-permute-start.1 = (f32[4,4,128]{2,1,0:T(4,128)S(1)}, f32[4,4,128]{2,1,0:T(4,128)S(1)}, u32[]{:S(2)}, u32[]{:S(2)}) collective-permute-start(f32[4,4,128]{2,1,0:T(4,128)S(1)} %get-tuple-element.25), channel_id=1, source_target_pairs={{0,2},{1,3},{2,0},{3,1},{4,6},{5,7},{6,4},{7,5},{8,10},{9,11},{10,... | collective-permute-start | bytes 24584 | tf_op jit(solution)/shard_map/ppermute | solution.py:668
  51.9 3.3 %collective-permute-start.2 = (f32[4,4,128]{2,1,0:T(4,128)S(1)}, f32[4,4,128]{2,1,0:T(4,128)S(1)}, u32[]{:S(2)}, u32[]{:S(2)}) collective-permute-start(f32[4,4,128]{2,1,0:T(4,128)S(1)} %get-tuple-element.26), channel_id=1, source_target_pairs={{0,3},{1,2},{2,1},{3,0},{4,7},{5,6},{6,5},{7,4},{8,11},{9,10},{10,... | collective-permute-start | bytes 24584 | tf_op jit(solution)/shard_map/ppermute | solution.py:668

commit v6 on v5

--- a/solution.py
+++ b/solution.py
@@ -48,7 +48,8 @@
 
 
 def pack_kernel(
-    rows_hbm, owner_hbm, mom_ref, out_ref, rows_ref, owner_ref, block_ref, sem, small_sem
+    rows_hbm, owner_hbm, mom_ref, out_ref,
+    rows_ref, owner_ref, block_ref, turned_ref, sem, small_sem, out_sem,
 ):
     small = [
         pltpu.make_async_copy(owner_hbm, owner_ref, small_sem.at[0]),
@@ -66,6 +67,17 @@
             )
     for copy in small + copies:
         copy.start()
+    leaving = []
+
+    def leave(t):
+        turned_ref[t] = block_ref[t * LANES : (t + 1) * LANES, :].T
+        leaving.append(
+            pltpu.make_async_copy(
+                turned_ref.at[t], out_ref.at[:, 0, pl.ds(t * LANES, LANES)], out_sem.at[t]
+            )
+        )
+        leaving[-1].start()
+
     for copy in small:
         copy.wait()
     owner_down = columns_down(owner_ref[...])
@@ -77,10 +89,15 @@
     for n in range(4):
         meta = jnp.where(which == n, rows_ref[n].astype(f32), meta)
     block_ref[META:, :] = meta
-    for copy in copies:
+    landed = 0
+    for t in range(ROWS1):
+        needed = min(-(-(t + 1) * LANES // LEV), CAP * DOWN)
+        for copy in copies[landed:needed]:
+            copy.wait()
+        landed = needed
+        leave(t)
+    for copy in leaving:
         copy.wait()
-    for t in range(ROWS1):
-        out_ref[pl.ds(t, PEERS, stride=ROWS1), :] = block_ref[t * LANES : (t + 1) * LANES, :].T
 
 
 def softplus(x):
@@ -373,6 +390,48 @@
 
     field = iota((FLD, LANES), 0)
     kept = (field >= 2) & (field <= 4)
+    copies = []
+    for h in range(COL // LANES):
+        for k in range(LEV):
+            rows = slice(k * FLD, (k + 1) * FLD)
+            at = slice(h * PAD_ROWS + k * PITCH, h * PAD_ROWS + k * PITCH + FLD)
+            mixed_state = jnp.where(kept, a_ref[at, :], y_ref[at, :])
+            tend_ref[h, rows, :] = mixed_state - tile_ref[h, rows, :]
+        copies.append(
+            pltpu.make_async_copy(
+                tend_ref.at[h], tend_out.at[:, pl.ds(h * LANES, LANES)], tend_sem.at[h]
+            )
+        )
+        copies[-1].start()
+
+    fields = jnp.concatenate(
+        [
+            jnp.concatenate(
+                [y_ref[pl.ds(h * PAD_ROWS + f, LEV, stride=PITCH), :] for f in (0, 1, 5, 6)], axis=0
+            )
+            for h in range(COL // LANES)
+        ],
+        axis=1,
+    )
+    parts = split2(fields)
+    sent = 0
+    for pair in range(CAP // 2):
+        hot = hot_ref[pair * 2 * PEERS : (pair + 1) * 2 * PEERS, :]
+        total = None
+        for part in parts:
+            got = lax.dot_general(
+                part, hot, (((1,), (1,)), ((), ())), preferred_element_type=f32
+            )
+            total = got if total is None else total + got
+        for q in range(2):
+            first = (pair * 2 + q) * UP * LEV
+            block_ref[first : first + UP * LEV, :] = total[:, q * PEERS : (q + 1) * PEERS]
+        ready = (pair + 1) * 2 * UP * LEV // LANES
+        for t in range(sent, ready):
+            out_ref[pl.ds(t, PEERS, stride=ROWS2), :] = block_ref[
+                t * LANES : (t + 1) * LANES, :
+            ].T
+        sent = ready
     bottom = []
     for h in range(COL // LANES):
         level = slice((LEV - 1) * FLD, LEV * FLD)
@@ -418,49 +477,6 @@
             other = products[n * 8 + e : n * 8 + e + 1, across : across + LANES]
             value = jnp.where(which == n, other, value)
         out_ref[pl.ds(ROWS_UP + e, PEERS, stride=ROWS2), :] = value
-
-    copies = []
-    for h in range(COL // LANES):
-        for k in range(LEV):
-            rows = slice(k * FLD, (k + 1) * FLD)
-            at = slice(h * PAD_ROWS + k * PITCH, h * PAD_ROWS + k * PITCH + FLD)
-            mixed_state = jnp.where(kept, a_ref[at, :], y_ref[at, :])
-            tend_ref[h, rows, :] = mixed_state - tile_ref[h, rows, :]
-        copies.append(
-            pltpu.make_async_copy(
-                tend_ref.at[h], tend_out.at[:, pl.ds(h * LANES, LANES)], tend_sem.at[h]
-            )
-        )
-        copies[-1].start()
-
-    fields = jnp.concatenate(
-        [
-            jnp.concatenate(
-                [y_ref[pl.ds(h * PAD_ROWS + f, LEV, stride=PITCH), :] for f in (0, 1, 5, 6)], axis=0
-            )
-            for h in range(COL // LANES)
-        ],
-        axis=1,
-    )
-    parts = split2(fields)
-    sent = 0
-    for pair in range(CAP // 2):
-        hot = hot_ref[pair * 2 * PEERS : (pair + 1) * 2 * PEERS, :]
-        total = None
-        for part in parts:
-            got = lax.dot_general(
-                part, hot, (((1,), (1,)), ((), ())), preferred_element_type=f32
-            )
-            total = got if total is None else total + got
-        for q in range(2):
-            first = (pair * 2 + q) * UP * LEV
-            block_ref[first : first + UP * LEV, :] = total[:, q * PEERS : (q + 1) * PEERS]
-        ready = (pair + 1) * 2 * UP * LEV // LANES
-        for t in range(sent, ready):
-            out_ref[pl.ds(t, PEERS, stride=ROWS2), :] = block_ref[
-                t * LANES : (t + 1) * LANES, :
-            ].T
-        sent = ready
     for copy in copies:
         copy.wait()
 
@@ -565,14 +581,16 @@
     return call(
         pack_kernel,
         [HBM] * 3,
-        [here((ROWS1 * PEERS, LANES))],
-        [VMEM],
+        [far((PEERS, 1, ROWS1 * LANES))],
+        [ANY],
         [
             pltpu.SMEM((4,), jnp.int32),
             pltpu.VMEM((1, COL), jnp.int32),
             pltpu.VMEM((ROWS1 * LANES, LANES), f32),
+            pltpu.VMEM((ROWS1, PEERS, LANES), f32),
             pltpu.SemaphoreType.DMA((CAP, DOWN)),
             pltpu.SemaphoreType.DMA((2,)),
+            pltpu.SemaphoreType.DMA((ROWS1,)),
         ],
     )(outside(rows), outside(owner_row), outside(mom))[0]
 

time: 56.1 us -> 56.4 us (level)
  no operation moved by 1% of the time
where the time goes in v6:
time: 56.4 us; the launch traced here: 56.2 us
  blocking collectives  21.6 us (38%)
  starting transfers between devices  14.5 us (26%)
  waiting for transfers between devices  10 us (18%)
  Pallas kernels  8.62 us (15%)
  between operations  0.74 us (1%)
  other arithmetic  0.6 us (1%)
    all_to_all x1, blocking collectives, exchange(): lax.all_to_all(sent.reshape(PEERS, 1, rows * LANES), ('node', 'dev'), 0,...  21.6 us
    all_to_all x1, starting transfers between devices, exchange(): lax.all_to_all(sent.reshape(PEERS, 1, rows * LANES), ('node', 'dev'), 0,...  11.5 us
    all_to_all x1, waiting for transfers between devices, exchange(): lax.all_to_all(sent.reshape(PEERS, 1, rows * LANES), ('node', 'dev'), 0,...  9.73 us
    pallas_call x1, Pallas kernels, physics(): call(physics_kernel, [SMEM] * 2 + [VMEM] * 6, [far((PLANE, COL)), here((R...  3.3 us
    ppermute x3, starting transfers between devices, local(): lax.ppermute(sums[flip], 'dev', [(i, i ^ flip) for i in range(dev_count)])  3.02 us
    pallas_call x1, Pallas kernels, pack(): call(pack_kernel, [HBM] * 3, [far((PEERS, 1, ROWS1 * LANES))], [ANY], [pl...  2.16 us
    pallas_call x1, Pallas kernels, prepare(): call(prepare_kernel, [VMEM] * 2 + [HBM] * 3, [here((2, PLANE, LANES)), he...  1.68 us
    pallas_call x1, Pallas kernels, update(): call(update_kernel, [VMEM] * 3, [far((PLANE, SLOTS))], [ANY], [pltpu.VMEM...  1.31 us
  transfers between devices with their start and end apart: 4, of which 2 were waited for; matrix products, arithmetic and copies ran while one was open for 0% of the time, Pallas kernels for 5%

profile of v6, /device:TPU:1, one launch (start us, length us, event | category | flops | bytes accessed | tf_op | source)
XLA Modules:
  0.0 56.2 jit_solution(6644786816502305197)
XLA Ops:
  0.6 0.0 copy-start.1
  0.6 0.0 copy-start
  0.7 2.2 %shard_map.94 = f32[128,1,640]{2,1,0:T(1,128)} custom-call(s32[4]{0:T(128)} %rows_hbm.1, s32[1,256]{1,0:T(1,128)} %bitcast.22, f32[72,8,512]{2,1,0:T(8,128)} %mom_ref.1), custom_call_target="tpu_custom_call" | custom-call | tf_op jit(solution)/shard_map/pallas_call | solution.py:581
  2.8 11.5 %all-to-all-start = ((f32[128,1,640]{2,1,0:T(1,128)}), f32[128,1,640]{2,1,0:T(1,128)S(1)}, u32[]{:S(2)}, u32[]{:S(2)}) async-start(f32[128,1,640]{2,1,0:T(1,128)} %shard_map.94), calls=%async_computation | async-start | bytes 655360 | tf_op jit(solution)/shard_map/all_to_all | solution.py:661
  14.3 0.0 copy-start.2
  14.3 0.0 copy-done.1
  14.3 0.0 copy-done
  14.4 1.7 %shard_map.95 = (f32[2,576,128]{2,1,0:T(8,128)S(1)}, bf16[512,256]{1,0:T(8,128)(2,1)S(1)}, f32[2,9,72,128]{3,2,1,0:T(8,128)S(1)}, f32[4,576,128]{2,1,0:T(8,128)S(1)}, bf16[2,256,256]{2,1,0:T(8,128)(2,1)S(1)}) custom-call(s32[1,256]{1,0:T(1,128)S(1)} %bitcast.23, s32[1,256]{1,0:T(1,128)S(1)} %bitcast.20, f32[576,256]{1,0:T(8,128)} %bitcast.26, ...), custom_call_target="tpu_custom_call" | custom-call | tf_op jit(solution)/shard_map/pallas_call | solution.py:599
  16.0 9.7 %all-to-all-done = f32[128,1,640]{2,1,0:T(1,128)S(1)} async-done(((f32[128,1,640]{2,1,0:T(1,128)}), f32[128,1,640]{2,1,0:T(1,128)S(1)}, u32[]{:S(2)}, u32[]{:S(2)}) %all-to-all-start) | async-done | bytes 327712 | tf_op jit(solution)/shard_map/all_to_all | solution.py:661
  25.8 0.0 copy-done.2
  25.8 3.3 %shard_map.96 = (f32[576,256]{1,0:T(8,128)}, f32[1664,128]{1,0:T(8,128)S(1)}, f32[24,128]{1,0:T(8,128)S(1)}) custom-call(s32[1]{0:T(128)} %bitcast.device_ref, s32[4]{0:T(128)S(1)} %copy-done.2, s32[1,256]{1,0:T(1,128)S(1)} %bitcast.21, f32[640,128]{1,0:T(8,128)S(1)} %bitcast.17, f32[2,576,128]{2,1,0:T(8,128)S(1)} %get-tuple-element.15.tile_ref, ...), custom_call_target="tpu_custom_call" | custom-call | tf_op jit(solution)/shard_map/pallas_call | solution.py:620
  29.1 21.6 %all_to_all.10 = f32[128,1,1664]{2,1,0:T(1,128)S(1)} all-to-all(f32[128,1,1664]{2,1,0:T(1,128)S(1)} %bitcast.18), channel_id=1, replica_groups=mesh['node'=4,'dev'=32] {'node','dev'}, dimensions={0} | all-to-all | bytes 1703936 | tf_op jit(solution)/shard_map/all_to_all | solution.py:661
  50.7 0.2 shard_map.98
  50.9 1.3 %collective-permute-start = (f32[4,4,128]{2,1,0:T(4,128)S(1)}, f32[4,4,128]{2,1,0:T(4,128)S(1)}, u32[]{:S(2)}, u32[]{:S(2)}) collective-permute-start(f32[4,4,128]{2,1,0:T(4,128)S(1)} %get-tuple-element.24), channel_id=1, source_target_pairs={{0,1},{1,0},{2,3},{3,2},{4,5},{5,4},{6,7},{7,6},{8,9},{9,8},{10,11... | collective-permute-start | bytes 24584 | tf_op jit(solution)/shard_map/ppermute | solution.py:686
  52.2 0.0 collective-permute-start.1
  52.2 1.7 %collective-permute-start.2 = (f32[4,4,128]{2,1,0:T(4,128)S(1)}, f32[4,4,128]{2,1,0:T(4,128)S(1)}, u32[]{:S(2)}, u32[]{:S(2)}) collective-permute-start(f32[4,4,128]{2,1,0:T(4,128)S(1)} %get-tuple-element.26), channel_id=1, source_target_pairs={{0,3},{1,2},{2,1},{3,0},{4,7},{5,6},{6,5},{7,4},{8,11},{9,10},{10,... | collective-permute-start | bytes 24584 | tf_op jit(solution)/shard_map/ppermute | solution.py:686
  53.9 1.3 %shard_map.97 = f32[576,512]{1,0:T(8,128)} custom-call(f32[24,128]{1,0:T(8,128)S(1)} %get-tuple-element.20.meta_ref, f32[1664,128]{1,0:T(8,128)S(1)} %bitcast.16, f32[4,576,128]{2,1,0:T(8,128)S(1)} %get-tuple-element.22.tile_ref), custom_call_target="tpu_custom_call" | custom-call | tf_op jit(solution)/shard_map/pallas_call | solution.py:647
  55.2 0.0 collective-permute-done
  55.3 0.0 collective-permute-done.1
  55.3 0.3 collective-permute-done.2
  55.6 0.6 %add_add_fusion = f32[2,8,128]{2,1,0:T(8,128)} fusion(f32[2,8,128]{2,1,0:T(8,128)S(1)} %bitcast.29, f32[2,8,128]{2,1,0:T(8,128)S(1)} %bitcast.28, f32[2,8,128]{2,1,0:T(8,128)S(1)} %bitcast.19, f32[2,8,128]{2,1,0:T(8,128)S(1)} %bitcast.27), kind=kLoop, calls=%fused_computation | loop fusion | flops 6144 | bytes 40960 | tf_op jit(solution)/shard_map/add | solution.py:688
Async XLA Ops:
  0.6 13.7 %copy-start.1 = (s32[256,1]{0,1:T(1,128)S(1)}, s32[256,1]{0,1:T(1,128)}, u32[]{:S(2)}) copy-start(s32[256,1]{0,1:T(1,128)} %param.8) | copy-start | bytes 3076
  0.6 13.7 %copy-start = (s32[256]{0:T(256)S(1)}, s32[256]{0:T(256)}, u32[]{:S(2)}) copy-start(s32[256]{0:T(256)} %param.9) | copy-start | bytes 3076
  2.8 23.0 %all-to-all-start = ((f32[128,1,640]{2,1,0:T(1,128)}), f32[128,1,640]{2,1,0:T(1,128)S(1)}, u32[]{:S(2)}, u32[]{:S(2)}) async-start(f32[128,1,640]{2,1,0:T(1,128)} %shard_map.94), calls=%async_computation | async-start | bytes 655360 | tf_op jit(solution)/shard_map/all_to_all | solution.py:661
  14.3 11.5 %copy-start.2 = (s32[4]{0:T(128)S(1)}, s32[4]{0:T(128)}, u32[]{:S(2)}) copy-start(s32[4]{0:T(128)} %cols_ref.1) | copy-start | bytes 52
  50.9 4.3 %collective-permute-start = (f32[4,4,128]{2,1,0:T(4,128)S(1)}, f32[4,4,128]{2,1,0:T(4,128)S(1)}, u32[]{:S(2)}, u32[]{:S(2)}) collective-permute-start(f32[4,4,128]{2,1,0:T(4,128)S(1)} %get-tuple-element.24), channel_id=1, source_target_pairs={{0,1},{1,0},{2,3},{3,2},{4,5},{5,4},{6,7},{7,6},{8,9},{9,8},{10,11... | collective-permute-start | bytes 24584 | tf_op jit(solution)/shard_map/ppermute | solution.py:686
  52.2 3.1 %collective-permute-start.1 = (f32[4,4,128]{2,1,0:T(4,128)S(1)}, f32[4,4,128]{2,1,0:T(4,128)S(1)}, u32[]{:S(2)}, u32[]{:S(2)}) collective-permute-start(f32[4,4,128]{2,1,0:T(4,128)S(1)} %get-tuple-element.25), channel_id=1, source_target_pairs={{0,2},{1,3},{2,0},{3,1},{4,6},{5,7},{6,4},{7,5},{8,10},{9,11},{10,... | collective-permute-start | bytes 24584 | tf_op jit(solution)/shard_map/ppermute | solution.py:686
  52.2 3.3 %collective-permute-start.2 = (f32[4,4,128]{2,1,0:T(4,128)S(1)}, f32[4,4,128]{2,1,0:T(4,128)S(1)}, u32[]{:S(2)}, u32[]{:S(2)}) collective-permute-start(f32[4,4,128]{2,1,0:T(4,128)S(1)} %get-tuple-element.26), channel_id=1, source_target_pairs={{0,3},{1,2},{2,1},{3,0},{4,7},{5,6},{6,5},{7,4},{8,11},{9,10},{10,... | collective-permute-start | bytes 24584 | tf_op jit(solution)/shard_map/ppermute | solution.py:686

commit v7 on v5

--- a/solution.py
+++ b/solution.py
@@ -103,9 +103,9 @@
     satur = 0.6 * jnp.exp(0.5 * half_t)
     excess = vapour - satur
     autoconv = 0.3 * liquid * liquid / (1.0 + liquid)
-    evapor = 0.1 * rain_q * (0.5 - 0.5 * jnp.tanh(0.5 * excess))
-    freeze = 0.3 * liquid * (0.5 - 0.5 * half_t)
-    melting = 0.2 * ice_q * (0.5 + 0.5 * half_t)
+    evapor = 0.05 * rain_q * (1.0 - jnp.tanh(0.5 * excess))
+    freeze = 0.15 * liquid * (1.0 - half_t)
+    melting = 0.1 * ice_q * (1.0 + half_t)
     aggreg = 0.25 * ice_q * ice_q / (1.0 + ice_q)
     source = jnp.where(
         icy, 0.175 * jnp.tanh(vapour - 0.8 * satur), 0.2 * jnp.tanh(excess)
@@ -156,9 +156,10 @@
 
     def finish(h, chain, step, r):
         k = LEV - 1 - step if chain else step
-        d = a_ref[rows(h, k), :] * r
+        d = a_ref[rows(h, k), :]
         if step > 0:
-            d = d + (link(h, chain, step) * r) * last_d[h, chain]
+            d = d + link(h, chain, step) * last_d[h, chain]
+        d = d * r
         g = row(k_ref, h, k - 1 if chain else k) * r
         g_ref[rows(h, k), :] = g
         y_ref[rows(h, k), :] = d
@@ -255,7 +256,7 @@
                     below = pltpu.roll(x[f], 7, 0)
                 square = (x[f] - below) * (x[f] - below)
                 shear = square if shear is None else shear + square
-            shear = 1.5 * shear / (1.0 + shear)
+            shear = 0.75 * shear / (1.0 + shear)
             values = kept[:3] + (rain, kept[4], source, excess, rain_q, shear)
             for f, value in enumerate(values):
                 part_ref[h, f, i * 8 : i * 8 + 8, :] = value
@@ -362,8 +363,8 @@
                 else:
                     du, dv = drop(5), drop(6)
                     shear = du * du + dv * dv
-                    shear = 1.5 * shear / (1.0 + shear)
-                mixing = 0.3 + shear * (0.5 - 0.5 * jnp.tanh(drop(0)))
+                    shear = 0.75 * shear / (1.0 + shear)
+                mixing = 0.3 + shear * (1.0 - jnp.tanh(drop(0)))
                 kappa = mixing * e_ref[i * 8 : i * 8 + 8, lanes]
                 rolled = pltpu.roll(kappa, 1, 0)
                 k_ref[i * 8 : i * 8 + 8, lanes] = kappa

time: 56.1 us -> 56.1 us (level)
  no operation moved by 1% of the time
where the time goes in v7:
time: 56.1 us; the launch traced here: 55.8 us
  blocking collectives  21.6 us (39%)
  starting transfers between devices  14.5 us (26%)
  waiting for transfers between devices  10 us (18%)
  Pallas kernels  8.28 us (15%)
  between operations  0.74 us (1%)
  other arithmetic  0.6 us (1%)
    all_to_all x1, blocking collectives, exchange(): lax.all_to_all(sent.reshape(PEERS, 1, rows * LANES), ('node', 'dev'), 0,...  21.6 us
    all_to_all x1, starting transfers between devices, exchange(): lax.all_to_all(sent.reshape(PEERS, 1, rows * LANES), ('node', 'dev'), 0,...  11.5 us
    all_to_all x1, waiting for transfers between devices, exchange(): lax.all_to_all(sent.reshape(PEERS, 1, rows * LANES), ('node', 'dev'), 0,...  9.73 us
    pallas_call x1, Pallas kernels, physics(): call(physics_kernel, [SMEM] * 2 + [VMEM] * 6, [far((PLANE, COL)), here((R...  3.16 us
    ppermute x3, starting transfers between devices, local(): lax.ppermute(sums[flip], 'dev', [(i, i ^ flip) for i in range(dev_count)])  3.02 us
    pallas_call x1, Pallas kernels, pack(): call(pack_kernel, [HBM] * 3, [here((ROWS1 * PEERS, LANES))], [VMEM], [plt...  1.95 us
    pallas_call x1, Pallas kernels, prepare(): call(prepare_kernel, [VMEM] * 2 + [HBM] * 3, [here((2, PLANE, LANES)), he...  1.67 us
    pallas_call x1, Pallas kernels, update(): call(update_kernel, [VMEM] * 3, [far((PLANE, SLOTS))], [ANY], [pltpu.VMEM...  1.31 us
  transfers between devices with their start and end apart: 4, of which 2 were waited for; matrix products, arithmetic and copies ran while one was open for 0% of the time, Pallas kernels for 5%

profile of v7, /device:TPU:1, one launch (start us, length us, event | category | flops | bytes accessed | tf_op | source)
XLA Modules:
  0.0 55.8 jit_solution(4363921547888772325)
XLA Ops:
  0.6 0.0 copy-start.1
  0.6 0.0 copy-start
  0.7 2.0 %shard_map.94 = f32[640,128]{1,0:T(8,128)} custom-call(s32[4]{0:T(128)} %rows_hbm.1, s32[1,256]{1,0:T(1,128)} %bitcast.23, f32[72,8,512]{2,1,0:T(8,128)} %mom_ref.1), custom_call_target="tpu_custom_call" | custom-call | tf_op jit(solution)/shard_map/pallas_call | solution.py:566
  2.6 11.5 %all-to-all-start = ((f32[128,1,640]{2,1,0:T(1,128)}), f32[128,1,640]{2,1,0:T(1,128)S(1)}, u32[]{:S(2)}, u32[]{:S(2)}) async-start(f32[128,1,640]{2,1,0:T(1,128)} %bitcast.3), calls=%async_computation | async-start | bytes 655360 | tf_op jit(solution)/shard_map/all_to_all | solution.py:644
  14.1 0.0 copy-start.2
  14.1 0.0 copy-done.1
  14.1 0.0 copy-done
  14.1 1.7 %shard_map.95 = (f32[2,576,128]{2,1,0:T(8,128)S(1)}, bf16[512,256]{1,0:T(8,128)(2,1)S(1)}, f32[2,9,72,128]{3,2,1,0:T(8,128)S(1)}, f32[4,576,128]{2,1,0:T(8,128)S(1)}, bf16[2,256,256]{2,1,0:T(8,128)(2,1)S(1)}) custom-call(s32[1,256]{1,0:T(1,128)S(1)} %bitcast.24, s32[1,256]{1,0:T(1,128)S(1)} %bitcast.21, f32[576,256]{1,0:T(8,128)} %bitcast.27, ...), custom_call_target="tpu_custom_call" | custom-call | tf_op jit(solution)/shard_map/pallas_call | solution.py:582
  15.8 9.7 %all-to-all-done = f32[128,1,640]{2,1,0:T(1,128)S(1)} async-done(((f32[128,1,640]{2,1,0:T(1,128)}), f32[128,1,640]{2,1,0:T(1,128)S(1)}, u32[]{:S(2)}, u32[]{:S(2)}) %all-to-all-start) | async-done | bytes 327712 | tf_op jit(solution)/shard_map/all_to_all | solution.py:644
  25.6 0.0 copy-done.2
  25.6 3.2 %shard_map.96 = (f32[576,256]{1,0:T(8,128)}, f32[1664,128]{1,0:T(8,128)S(1)}, f32[24,128]{1,0:T(8,128)S(1)}) custom-call(s32[1]{0:T(128)} %bitcast.device_ref, s32[4]{0:T(128)S(1)} %copy-done.2, s32[1,256]{1,0:T(1,128)S(1)} %bitcast.22, f32[640,128]{1,0:T(8,128)S(1)} %bitcast.18, f32[2,576,128]{2,1,0:T(8,128)S(1)} %get-tuple-element.15.tile_ref, ...), custom_call_target="tpu_custom_call" | custom-call | tf_op jit(solution)/shard_map/pallas_call | solution.py:603
  28.7 21.6 %all_to_all.10 = f32[128,1,1664]{2,1,0:T(1,128)S(1)} all-to-all(f32[128,1,1664]{2,1,0:T(1,128)S(1)} %bitcast.19), channel_id=1, replica_groups=mesh['node'=4,'dev'=32] {'node','dev'}, dimensions={0} | all-to-all | bytes 1703936 | tf_op jit(solution)/shard_map/all_to_all | solution.py:644
  50.4 0.2 shard_map.98
  50.6 1.3 %collective-permute-start = (f32[4,4,128]{2,1,0:T(4,128)S(1)}, f32[4,4,128]{2,1,0:T(4,128)S(1)}, u32[]{:S(2)}, u32[]{:S(2)}) collective-permute-start(f32[4,4,128]{2,1,0:T(4,128)S(1)} %get-tuple-element.24), channel_id=1, source_target_pairs={{0,1},{1,0},{2,3},{3,2},{4,5},{5,4},{6,7},{7,6},{8,9},{9,8},{10,11... | collective-permute-start | bytes 24584 | tf_op jit(solution)/shard_map/ppermute | solution.py:669
  51.9 0.0 collective-permute-start.1
  51.9 1.7 %collective-permute-start.2 = (f32[4,4,128]{2,1,0:T(4,128)S(1)}, f32[4,4,128]{2,1,0:T(4,128)S(1)}, u32[]{:S(2)}, u32[]{:S(2)}) collective-permute-start(f32[4,4,128]{2,1,0:T(4,128)S(1)} %get-tuple-element.26), channel_id=1, source_target_pairs={{0,3},{1,2},{2,1},{3,0},{4,7},{5,6},{6,5},{7,4},{8,11},{9,10},{10,... | collective-permute-start | bytes 24584 | tf_op jit(solution)/shard_map/ppermute | solution.py:669
  53.6 1.3 %shard_map.97 = f32[576,512]{1,0:T(8,128)} custom-call(f32[24,128]{1,0:T(8,128)S(1)} %get-tuple-element.20.meta_ref, f32[1664,128]{1,0:T(8,128)S(1)} %bitcast.17, f32[4,576,128]{2,1,0:T(8,128)S(1)} %get-tuple-element.22.tile_ref), custom_call_target="tpu_custom_call" | custom-call | tf_op jit(solution)/shard_map/pallas_call | solution.py:630
  54.9 0.0 collective-permute-done
  54.9 0.0 collective-permute-done.1
  54.9 0.3 collective-permute-done.2
  55.2 0.6 %add_add_fusion = f32[2,8,128]{2,1,0:T(8,128)} fusion(f32[2,8,128]{2,1,0:T(8,128)S(1)} %bitcast.30, f32[2,8,128]{2,1,0:T(8,128)S(1)} %bitcast.29, f32[2,8,128]{2,1,0:T(8,128)S(1)} %bitcast.20, f32[2,8,128]{2,1,0:T(8,128)S(1)} %bitcast.28), kind=kLoop, calls=%fused_computation | loop fusion | flops 6144 | bytes 40960 | tf_op jit(solution)/shard_map/add | solution.py:671
Async XLA Ops:
  0.6 13.5 %copy-start.1 = (s32[256,1]{0,1:T(1,128)S(1)}, s32[256,1]{0,1:T(1,128)}, u32[]{:S(2)}) copy-start(s32[256,1]{0,1:T(1,128)} %param.8) | copy-start | bytes 3076
  0.6 13.5 %copy-start = (s32[256]{0:T(256)S(1)}, s32[256]{0:T(256)}, u32[]{:S(2)}) copy-start(s32[256]{0:T(256)} %param.9) | copy-start | bytes 3076
  2.6 23.0 %all-to-all-start = ((f32[128,1,640]{2,1,0:T(1,128)}), f32[128,1,640]{2,1,0:T(1,128)S(1)}, u32[]{:S(2)}, u32[]{:S(2)}) async-start(f32[128,1,640]{2,1,0:T(1,128)} %bitcast.3), calls=%async_computation | async-start | bytes 655360 | tf_op jit(solution)/shard_map/all_to_all | solution.py:644
  14.1 11.5 %copy-start.2 = (s32[4]{0:T(128)S(1)}, s32[4]{0:T(128)}, u32[]{:S(2)}) copy-start(s32[4]{0:T(128)} %cols_ref.1) | copy-start | bytes 52
  50.6 4.3 %collective-permute-start = (f32[4,4,128]{2,1,0:T(4,128)S(1)}, f32[4,4,128]{2,1,0:T(4,128)S(1)}, u32[]{:S(2)}, u32[]{:S(2)}) collective-permute-start(f32[4,4,128]{2,1,0:T(4,128)S(1)} %get-tuple-element.24), channel_id=1, source_target_pairs={{0,1},{1,0},{2,3},{3,2},{4,5},{5,4},{6,7},{7,6},{8,9},{9,8},{10,11... | collective-permute-start | bytes 24584 | tf_op jit(solution)/shard_map/ppermute | solution.py:669
  51.9 3.1 %collective-permute-start.1 = (f32[4,4,128]{2,1,0:T(4,128)S(1)}, f32[4,4,128]{2,1,0:T(4,128)S(1)}, u32[]{:S(2)}, u32[]{:S(2)}) collective-permute-start(f32[4,4,128]{2,1,0:T(4,128)S(1)} %get-tuple-element.25), channel_id=1, source_target_pairs={{0,2},{1,3},{2,0},{3,1},{4,6},{5,7},{6,4},{7,5},{8,10},{9,11},{10,... | collective-permute-start | bytes 24584 | tf_op jit(solution)/shard_map/ppermute | solution.py:669
  51.9 3.3 %collective-permute-start.2 = (f32[4,4,128]{2,1,0:T(4,128)S(1)}, f32[4,4,128]{2,1,0:T(4,128)S(1)}, u32[]{:S(2)}, u32[]{:S(2)}) collective-permute-start(f32[4,4,128]{2,1,0:T(4,128)S(1)} %get-tuple-element.26), channel_id=1, source_target_pairs={{0,3},{1,2},{2,1},{3,0},{4,7},{5,6},{6,5},{7,4},{8,11},{9,10},{10,... | collective-permute-start | bytes 24584 | tf_op jit(solution)/shard_map/ppermute | solution.py:669

commit v8 on v5

--- a/solution.py
+++ b/solution.py
@@ -64,7 +64,7 @@
                     sem.at[p, at],
                 )
             )
-    for copy in small + copies:
+    for copy in copies + small:
         copy.start()
     for copy in small:
         copy.wait()
@@ -156,9 +156,10 @@
 
     def finish(h, chain, step, r):
         k = LEV - 1 - step if chain else step
-        d = a_ref[rows(h, k), :] * r
+        d = a_ref[rows(h, k), :]
         if step > 0:
-            d = d + (link(h, chain, step) * r) * last_d[h, chain]
+            d = d + link(h, chain, step) * last_d[h, chain]
+        d = d * r
         g = row(k_ref, h, k - 1 if chain else k) * r
         g_ref[rows(h, k), :] = g
         y_ref[rows(h, k), :] = d

time: 56.1 us -> 56.1 us (level)
  no operation moved by 1% of the time
where the time goes in v8:
time: 56.1 us; the launch traced here: 55.9 us
  blocking collectives  21.6 us (39%)
  starting transfers between devices  14.5 us (26%)
  waiting for transfers between devices  10 us (18%)
  Pallas kernels  8.31 us (15%)
  between operations  0.74 us (1%)
  other arithmetic  0.6 us (1%)
    all_to_all x1, blocking collectives, exchange(): lax.all_to_all(sent.reshape(PEERS, 1, rows * LANES), ('node', 'dev'), 0,...  21.6 us
    all_to_all x1, starting transfers between devices, exchange(): lax.all_to_all(sent.reshape(PEERS, 1, rows * LANES), ('node', 'dev'), 0,...  11.5 us
    all_to_all x1, waiting for transfers between devices, exchange(): lax.all_to_all(sent.reshape(PEERS, 1, rows * LANES), ('node', 'dev'), 0,...  9.73 us
    pallas_call x1, Pallas kernels, physics(): call(physics_kernel, [SMEM] * 2 + [VMEM] * 6, [far((PLANE, COL)), here((R...  3.17 us
    ppermute x3, starting transfers between devices, local(): lax.ppermute(sums[flip], 'dev', [(i, i ^ flip) for i in range(dev_count)])  3.02 us
    pallas_call x1, Pallas kernels, pack(): call(pack_kernel, [HBM] * 3, [here((ROWS1 * PEERS, LANES))], [VMEM], [plt...  1.98 us
    pallas_call x1, Pallas kernels, prepare(): call(prepare_kernel, [VMEM] * 2 + [HBM] * 3, [here((2, PLANE, LANES)), he...  1.68 us
    pallas_call x1, Pallas kernels, update(): call(update_kernel, [VMEM] * 3, [far((PLANE, SLOTS))], [ANY], [pltpu.VMEM...  1.31 us
  transfers between devices with their start and end apart: 4, of which 2 were waited for; matrix products, arithmetic and copies ran while one was open for 0% of the time, Pallas kernels for 5%

profile of v8, /device:TPU:1, one launch (start us, length us, event | category | flops | bytes accessed | tf_op | source)
XLA Modules:
  0.0 55.9 jit_solution(11783877285621686120)
XLA Ops:
  0.6 0.0 copy-start.1
  0.6 0.0 copy-start
  0.7 2.0 %shard_map.94 = f32[640,128]{1,0:T(8,128)} custom-call(s32[4]{0:T(128)} %rows_hbm.1, s32[1,256]{1,0:T(1,128)} %bitcast.23, f32[72,8,512]{2,1,0:T(8,128)} %mom_ref.1), custom_call_target="tpu_custom_call" | custom-call | tf_op jit(solution)/shard_map/pallas_call | solution.py:566
  2.6 11.5 %all-to-all-start = ((f32[128,1,640]{2,1,0:T(1,128)}), f32[128,1,640]{2,1,0:T(1,128)S(1)}, u32[]{:S(2)}, u32[]{:S(2)}) async-start(f32[128,1,640]{2,1,0:T(1,128)} %bitcast.3), calls=%async_computation | async-start | bytes 655360 | tf_op jit(solution)/shard_map/all_to_all | solution.py:644
  14.1 0.0 copy-start.2
  14.2 0.0 copy-done.1
  14.2 0.0 copy-done
  14.2 1.7 %shard_map.95 = (f32[2,576,128]{2,1,0:T(8,128)S(1)}, bf16[512,256]{1,0:T(8,128)(2,1)S(1)}, f32[2,9,72,128]{3,2,1,0:T(8,128)S(1)}, f32[4,576,128]{2,1,0:T(8,128)S(1)}, bf16[2,256,256]{2,1,0:T(8,128)(2,1)S(1)}) custom-call(s32[1,256]{1,0:T(1,128)S(1)} %bitcast.24, s32[1,256]{1,0:T(1,128)S(1)} %bitcast.21, f32[576,256]{1,0:T(8,128)} %bitcast.27, ...), custom_call_target="tpu_custom_call" | custom-call | tf_op jit(solution)/shard_map/pallas_call | solution.py:582
  15.9 9.7 %all-to-all-done = f32[128,1,640]{2,1,0:T(1,128)S(1)} async-done(((f32[128,1,640]{2,1,0:T(1,128)}), f32[128,1,640]{2,1,0:T(1,128)S(1)}, u32[]{:S(2)}, u32[]{:S(2)}) %all-to-all-start) | async-done | bytes 327712 | tf_op jit(solution)/shard_map/all_to_all | solution.py:644
  25.6 0.0 copy-done.2
  25.6 3.2 %shard_map.96 = (f32[576,256]{1,0:T(8,128)}, f32[1664,128]{1,0:T(8,128)S(1)}, f32[24,128]{1,0:T(8,128)S(1)}) custom-call(s32[1]{0:T(128)} %bitcast.device_ref, s32[4]{0:T(128)S(1)} %copy-done.2, s32[1,256]{1,0:T(1,128)S(1)} %bitcast.22, f32[640,128]{1,0:T(8,128)S(1)} %bitcast.18, f32[2,576,128]{2,1,0:T(8,128)S(1)} %get-tuple-element.15.tile_ref, ...), custom_call_target="tpu_custom_call" | custom-call | tf_op jit(solution)/shard_map/pallas_call | solution.py:603
  28.8 21.6 %all_to_all.10 = f32[128,1,1664]{2,1,0:T(1,128)S(1)} all-to-all(f32[128,1,1664]{2,1,0:T(1,128)S(1)} %bitcast.19), channel_id=1, replica_groups=mesh['node'=4,'dev'=32] {'node','dev'}, dimensions={0} | all-to-all | bytes 1703936 | tf_op jit(solution)/shard_map/all_to_all | solution.py:644
  50.4 0.2 shard_map.98
  50.6 1.3 %collective-permute-start = (f32[4,4,128]{2,1,0:T(4,128)S(1)}, f32[4,4,128]{2,1,0:T(4,128)S(1)}, u32[]{:S(2)}, u32[]{:S(2)}) collective-permute-start(f32[4,4,128]{2,1,0:T(4,128)S(1)} %get-tuple-element.24), channel_id=1, source_target_pairs={{0,1},{1,0},{2,3},{3,2},{4,5},{5,4},{6,7},{7,6},{8,9},{9,8},{10,11... | collective-permute-start | bytes 24584 | tf_op jit(solution)/shard_map/ppermute | solution.py:669
  51.9 0.0 collective-permute-start.1
  51.9 1.7 %collective-permute-start.2 = (f32[4,4,128]{2,1,0:T(4,128)S(1)}, f32[4,4,128]{2,1,0:T(4,128)S(1)}, u32[]{:S(2)}, u32[]{:S(2)}) collective-permute-start(f32[4,4,128]{2,1,0:T(4,128)S(1)} %get-tuple-element.26), channel_id=1, source_target_pairs={{0,3},{1,2},{2,1},{3,0},{4,7},{5,6},{6,5},{7,4},{8,11},{9,10},{10,... | collective-permute-start | bytes 24584 | tf_op jit(solution)/shard_map/ppermute | solution.py:669
  53.6 1.3 %shard_map.97 = f32[576,512]{1,0:T(8,128)} custom-call(f32[24,128]{1,0:T(8,128)S(1)} %get-tuple-element.20.meta_ref, f32[1664,128]{1,0:T(8,128)S(1)} %bitcast.17, f32[4,576,128]{2,1,0:T(8,128)S(1)} %get-tuple-element.22.tile_ref), custom_call_target="tpu_custom_call" | custom-call | tf_op jit(solution)/shard_map/pallas_call | solution.py:630
  54.9 0.0 collective-permute-done
  55.0 0.0 collective-permute-done.1
  55.0 0.3 collective-permute-done.2
  55.2 0.6 %add_add_fusion = f32[2,8,128]{2,1,0:T(8,128)} fusion(f32[2,8,128]{2,1,0:T(8,128)S(1)} %bitcast.30, f32[2,8,128]{2,1,0:T(8,128)S(1)} %bitcast.29, f32[2,8,128]{2,1,0:T(8,128)S(1)} %bitcast.20, f32[2,8,128]{2,1,0:T(8,128)S(1)} %bitcast.28), kind=kLoop, calls=%fused_computation | loop fusion | flops 6144 | bytes 40960 | tf_op jit(solution)/shard_map/add | solution.py:671
Async XLA Ops:
  0.6 13.5 %copy-start.1 = (s32[256,1]{0,1:T(1,128)S(1)}, s32[256,1]{0,1:T(1,128)}, u32[]{:S(2)}) copy-start(s32[256,1]{0,1:T(1,128)} %param.8) | copy-start | bytes 3076
  0.6 13.5 %copy-start = (s32[256]{0:T(256)S(1)}, s32[256]{0:T(256)}, u32[]{:S(2)}) copy-start(s32[256]{0:T(256)} %param.9) | copy-start | bytes 3076
  2.6 23.0 %all-to-all-start = ((f32[128,1,640]{2,1,0:T(1,128)}), f32[128,1,640]{2,1,0:T(1,128)S(1)}, u32[]{:S(2)}, u32[]{:S(2)}) async-start(f32[128,1,640]{2,1,0:T(1,128)} %bitcast.3), calls=%async_computation | async-start | bytes 655360 | tf_op jit(solution)/shard_map/all_to_all | solution.py:644
  14.1 11.5 %copy-start.2 = (s32[4]{0:T(128)S(1)}, s32[4]{0:T(128)}, u32[]{:S(2)}) copy-start(s32[4]{0:T(128)} %cols_ref.1) | copy-start | bytes 52
  50.6 4.3 %collective-permute-start = (f32[4,4,128]{2,1,0:T(4,128)S(1)}, f32[4,4,128]{2,1,0:T(4,128)S(1)}, u32[]{:S(2)}, u32[]{:S(2)}) collective-permute-start(f32[4,4,128]{2,1,0:T(4,128)S(1)} %get-tuple-element.24), channel_id=1, source_target_pairs={{0,1},{1,0},{2,3},{3,2},{4,5},{5,4},{6,7},{7,6},{8,9},{9,8},{10,11... | collective-permute-start | bytes 24584 | tf_op jit(solution)/shard_map/ppermute | solution.py:669
  51.9 3.1 %collective-permute-start.1 = (f32[4,4,128]{2,1,0:T(4,128)S(1)}, f32[4,4,128]{2,1,0:T(4,128)S(1)}, u32[]{:S(2)}, u32[]{:S(2)}) collective-permute-start(f32[4,4,128]{2,1,0:T(4,128)S(1)} %get-tuple-element.25), channel_id=1, source_target_pairs={{0,2},{1,3},{2,0},{3,1},{4,6},{5,7},{6,4},{7,5},{8,10},{9,11},{10,... | collective-permute-start | bytes 24584 | tf_op jit(solution)/shard_map/ppermute | solution.py:669
  51.9 3.3 %collective-permute-start.2 = (f32[4,4,128]{2,1,0:T(4,128)S(1)}, f32[4,4,128]{2,1,0:T(4,128)S(1)}, u32[]{:S(2)}, u32[]{:S(2)}) collective-permute-start(f32[4,4,128]{2,1,0:T(4,128)S(1)} %get-tuple-element.26), channel_id=1, source_target_pairs={{0,3},{1,2},{2,1},{3,0},{4,7},{5,6},{6,5},{7,4},{8,11},{9,10},{10,... | collective-permute-start | bytes 24584 | tf_op jit(solution)/shard_map/ppermute | solution.py:669
